TPU v7x, 512 devices: a whole 4x4x16 slice. The times are simulated.
512 devices in a mesh: rows: 64 (over x_lo, z, core), blk: 8 (over x_hi, y).
Axes of the slice: x: 4 (x_hi: 2, x_lo: 2; x = x_hi * 2 + x_lo), y: 4, z: 16, core: 2. Of those that a mesh axis runs over, the one named last changes fastest.
Arguments:
- cov_blocks: bfloat16 [1024, 40, 128, 128], P(('rows', 'blk')), may hold values from -24 to 24
- col_index: int32 [1024, 40], P(('rows', 'blk')), may hold values from 0 to 1023, as said below
- block_count: int32 [1024], P(('rows', 'blk')), may hold values from 2 to 40, as said below
- probes: bfloat16 [131072, 512], P(('rows', 'blk')), may hold values from -60 to 60
Outputs:
- basis: float32 [131072, 512], P(('rows', 'blk'))
Inputs may be any that keep to these rules, and one draw needn't show every extreme that they name: `col_index`: the live slots of block row i name distinct column blocks of zone i // 16 or of an adjacent zone; rows of the first and last zone have at most 32 live slots; every entry of a row is distinct. `block_count`: some block row uses all 40 slots in every draw.
All inputs are finite; a program needn't handle non-finite values.
Results may differ from a plain program's by a relative error of at most 0.0003.
Values may be sent and summed in bfloat16 or wider, within the bound.
A program may use at most 64 MiB of HBM per device.

v0:
```python
import functools
import jax
import jax.numpy as jnp
from jax import lax
from jax.experimental import pallas as pl
from jax.experimental.pallas import tpu as pltpu
from jax.sharding import PartitionSpec as P

MESH_ID = pl.DeviceIdType.MESH


def _ar_kernel(dims, g_ref, out_ref, rc, ry, rx, rzl, rzh, a1, a2, a3, a4, full, ssem, rsem):
    XL, Z, C, XH, Y = dims
    X = XL * XH
    ZH = Z // 2
    N = g_ref.shape[0]
    S1 = N // C
    S2 = S1 // Y
    S3 = S2 // X
    S4 = S3 // 2
    r = lax.axis_index("rows")
    b = lax.axis_index("blk")
    c = r % C
    z = (r // C) % Z
    xl = r // (C * Z)
    xh = b // Y
    y = b % Y
    x = xh * XL + xl
    zl = z % 2
    zh = z // 2

    def dev(c_, y_, x_, z_):
        return ((x_ % XL) * (Z * C) + z_ * C + c_, (x_ // XL) * Y + y_)

    core_peer = dev(1 - c, y, x, z)
    y_peers = [(y + k) % Y for k in range(1, Y)]
    x_peers = [(x + k) % X for k in range(1, X)]
    zl_peer = dev(c, y, x, zh * 2 + 1 - zl)
    zh_peers = [(zh + k) % ZH for k in range(1, ZH)]
    peers = [core_peer, zl_peer]
    peers += [dev(c, p, x, z) for p in y_peers]
    peers += [dev(c, y, p, z) for p in x_peers]
    peers += [dev(c, y, x, p * 2 + zl) for p in zh_peers]

    barrier = pltpu.get_barrier_semaphore()
    for p in peers:
        pl.semaphore_signal(barrier, inc=1, device_id=p, device_id_type=MESH_ID)
    pl.semaphore_wait(barrier, len(peers))

    o_core, o_y, o_x, o_zl, o_zh = 0, 1, 1 + Y, 1 + Y + X, 2 + Y + X
    o_agzl, o_agx, o_agy, o_agc = 2 + Y + X + ZH, 3 + Y + X + ZH, 3 + Y + 2 * X + ZH, 3 + 2 * Y + 2 * X + ZH

    def send(src, dst, sidx, ridx, peer):
        d = pltpu.make_async_remote_copy(
            src_ref=src, dst_ref=dst, send_sem=ssem.at[sidx], recv_sem=rsem.at[ridx],
            device_id=peer, device_id_type=MESH_ID)
        d.start()
        return d

    def wait_recv(src, dst, ridx, peer):
        pltpu.make_async_remote_copy(
            src_ref=src, dst_ref=dst, send_sem=ssem.at[0], recv_sem=rsem.at[ridx],
            device_id=peer, device_id_type=MESH_ID).wait_recv()

    def rows(start, size):
        return pl.ds(pl.multiple_of(start, 8), size)

    d = send(g_ref.at[rows((1 - c) * S1, S1)], rc, o_core, o_core, core_peer)
    wait_recv(g_ref.at[rows(c * S1, S1)], rc, o_core, core_peer)
    d.wait_send()
    a1[...] = g_ref[rows(c * S1, S1), :] + rc[...]

    ds = [send(a1.at[rows(p * S2, S2)], ry.at[y], o_y + k, o_y + y, dev(c, p, x, z))
          for k, p in enumerate(y_peers)]
    for k in range(1, Y):
        s = (y - k + Y) % Y
        wait_recv(a1.at[rows(0, S2)], ry.at[s], o_y + s, dev(c, s, x, z))
    for d in ds:
        d.wait_send()
    acc = a1[rows(y * S2, S2), :]
    for k in range(1, Y):
        acc = acc + ry[(y - k + Y) % Y]
    a2[...] = acc

    ds = [send(a2.at[rows(p * S3, S3)], rx.at[x], o_x + k, o_x + x, dev(c, y, p, z))
          for k, p in enumerate(x_peers)]
    for k in range(1, X):
        s = (x - k + X) % X
        wait_recv(a2.at[rows(0, S3)], rx.at[s], o_x + s, dev(c, y, s, z))
    for d in ds:
        d.wait_send()
    acc = a2[rows(x * S3, S3), :]
    for k in range(1, X):
        acc = acc + rx[(x - k + X) % X]
    a3[...] = acc

    d = send(a3.at[rows((1 - zl) * S4, S4)], rzl, o_zl, o_zl, zl_peer)
    wait_recv(a3.at[rows(zl * S4, S4)], rzl, o_zl, zl_peer)
    d.wait_send()
    a4[...] = a3[rows(zl * S4, S4), :] + rzl[...]

    ds = [send(a4, rzh.at[zh], o_zh + k, o_zh + zh, dev(c, y, x, p * 2 + zl))
          for k, p in enumerate(zh_peers)]
    rzh[zh] = a4[...]
    for k in range(1, ZH):
        s = (zh - k + ZH) % ZH
        wait_recv(a4, rzh.at[s], o_zh + s, dev(c, y, x, s * 2 + zl))
    for d in ds:
        d.wait_send()
    acc = rzh[0]
    for j in range(1, ZH):
        acc = acc + rzh[j]
    base = c * S1 + y * S2 + x * S3
    full[rows(base + zl * S4, S4), :] = acc

    mine = rows(base + zl * S4, S4)
    d = send(full.at[mine], full.at[mine], o_agzl, o_agzl, zl_peer)
    wait_recv(full.at[mine], full.at[rows(base + (1 - zl) * S4, S4)], o_agzl, zl_peer)
    d.wait_send()

    mine = rows(c * S1 + y * S2 + x * S3, S3)
    ds = [send(full.at[mine], full.at[mine], o_agx + k, o_agx + x, dev(c, y, p, z))
          for k, p in enumerate(x_peers)]
    for k in range(1, X):
        s = (x - k + X) % X
        wait_recv(full.at[mine], full.at[rows(c * S1 + y * S2 + s * S3, S3)], o_agx + s, dev(c, y, s, z))
    for d in ds:
        d.wait_send()

    mine = rows(c * S1 + y * S2, S2)
    ds = [send(full.at[mine], full.at[mine], o_agy + k, o_agy + y, dev(c, p, x, z))
          for k, p in enumerate(y_peers)]
    for k in range(1, Y):
        s = (y - k + Y) % Y
        wait_recv(full.at[mine], full.at[rows(c * S1 + s * S2, S2)], o_agy + s, dev(c, s, x, z))
    for d in ds:
        d.wait_send()

    mine = rows(c * S1, S1)
    d = send(full.at[mine], full.at[mine], o_agc, o_agc, core_peer)
    wait_recv(full.at[mine], full.at[rows((1 - c) * S1, S1)], o_agc, core_peer)
    d.wait_send()

    out_ref[...] = full[...]


def _zone_gather_kernel(nb, p_ref, out_ref, ssem, rsem, lsem):
    T = p_ref.shape[0]
    r = lax.axis_index("rows")
    b = lax.axis_index("blk")
    barrier = pltpu.get_barrier_semaphore()
    for k in range(1, nb):
        pl.semaphore_signal(barrier, inc=1, device_id=(r, (b + k) % nb), device_id_type=MESH_ID)
    pl.semaphore_wait(barrier, nb - 1)
    here = pl.ds(pl.multiple_of(b * T, 8), T)
    ds = []
    for k in range(1, nb):
        d = pltpu.make_async_remote_copy(
            src_ref=p_ref, dst_ref=out_ref.at[here], send_sem=ssem.at[k - 1], recv_sem=rsem.at[b],
            device_id=(r, (b + k) % nb), device_id_type=MESH_ID)
        d.start()
        ds.append(d)
    own = pltpu.make_async_copy(p_ref, out_ref.at[here], lsem.at[0])
    own.start()
    for k in range(1, nb):
        s = (b - k + nb) % nb
        pltpu.make_async_remote_copy(
            src_ref=p_ref, dst_ref=out_ref.at[pl.ds(pl.multiple_of(s * T, 8), T)], send_sem=ssem.at[0],
            recv_sem=rsem.at[s], device_id=(r, s), device_id_type=MESH_ID).wait_recv()
    for d in ds:
        d.wait_send()
    own.wait()


def zone_gather(p, nb):
    T, K = p.shape
    return pl.pallas_call(
        functools.partial(_zone_gather_kernel, nb),
        out_shape=jax.ShapeDtypeStruct((nb * T, K), p.dtype),
        in_specs=[pl.BlockSpec(memory_space=pl.ANY)],
        out_specs=pl.BlockSpec(memory_space=pl.ANY),
        scratch_shapes=[
            pltpu.SemaphoreType.DMA((nb - 1,)),
            pltpu.SemaphoreType.DMA((nb,)),
            pltpu.SemaphoreType.DMA((1,)),
        ],
        compiler_params=pltpu.CompilerParams(collective_id=1, has_side_effects=True),
    )(p)


HI = lax.Precision.HIGHEST


def _mm(a, b):
    return jnp.dot(a, b, precision=HI, preferred_element_type=jnp.float32)


def _mm_t(a, b):
    return lax.dot_general(a, b, (((1,), (1,)), ((), ())), precision=HI, preferred_element_type=jnp.float32)


def _chol_inv_kernel(g_ref, m_ref, a_ref, d_ref, b_ref, l_ref):
    n = g_ref.shape[0]
    t = d_ref.shape[0]
    nb = n // t
    a_ref[...] = g_ref[...]
    m_ref[...] = jnp.zeros_like(m_ref)
    lane = lax.broadcasted_iota(jnp.int32, (1, t), 1)
    lane2 = lax.broadcasted_iota(jnp.int32, (t, t), 1)
    sub = lax.broadcasted_iota(jnp.int32, (t, 1), 0)
    eye = (lax.broadcasted_iota(jnp.int32, (t, t), 0) == lane2).astype(jnp.float32)

    def step(j, carry):
        row = d_ref[pl.ds(j, 1), :]
        piv2 = jnp.sum(jnp.where(lane == j, row, 0.0), axis=1, keepdims=True)
        inv = 1.0 / jnp.sqrt(piv2)
        dmat = d_ref[...]
        colfull = jnp.sum(jnp.where(lane2 == j, dmat, 0.0), axis=1, keepdims=True)
        col = jnp.where(sub >= j, colfull * inv, 0.0)
        lrow = jnp.where(lane >= j, row * inv, 0.0)
        d_ref[...] = dmat - col * lrow
        brow = b_ref[pl.ds(j, 1), :] * inv
        bmat = b_ref[...]
        b_ref[...] = bmat - jnp.where(sub > j, col, 0.0) * brow
        b_ref[pl.ds(j, 1), :] = brow
        return carry

    for k in range(nb):
        lo = k * t
        d_ref[...] = a_ref[lo:lo + t, lo:lo + t]
        b_ref[...] = eye
        lax.fori_loop(0, t, step, 0)
        m_ref[lo:lo + t, lo:lo + t] = b_ref[...]
        if k < nb - 1:
            hi = lo + t
            panel = _mm_t(a_ref[hi:, lo:lo + t], b_ref[...])
            l_ref[hi:, lo:lo + t] = panel
            a_ref[hi:, hi:] = a_ref[hi:, hi:] - _mm_t(panel, panel)
    for dist in range(1, nb):
        for i in range(dist, nb):
            j = i - dist
            acc = None
            for k in range(j, i):
                term = _mm(l_ref[i * t:(i + 1) * t, k * t:(k + 1) * t], m_ref[k * t:(k + 1) * t, j * t:(j + 1) * t])
                acc = term if acc is None else acc + term
            m_ref[i * t:(i + 1) * t, j * t:(j + 1) * t] = -_mm(m_ref[i * t:(i + 1) * t, i * t:(i + 1) * t], acc)


def chol_inverse(g, t=128):
    n = g.shape[0]
    vmem = pltpu.VMEM
    return pl.pallas_call(
        _chol_inv_kernel,
        out_shape=jax.ShapeDtypeStruct((n, n), jnp.float32),
        in_specs=[pl.BlockSpec(memory_space=vmem)],
        out_specs=pl.BlockSpec(memory_space=vmem),
        scratch_shapes=[
            vmem((n, n), jnp.float32),
            vmem((t, t), jnp.float32),
            vmem((t, t), jnp.float32),
            vmem((n, n), jnp.float32),
        ],
    )(g)


def gram_allreduce(g, dims):
    XL, Z, C, XH, Y = dims
    X = XL * XH
    ZH = Z // 2
    N, M = g.shape
    S1 = N // C
    S2 = S1 // Y
    S3 = S2 // X
    S4 = S3 // 2
    nsem = 4 + 2 * Y + 2 * X + ZH
    vmem = pltpu.VMEM
    return pl.pallas_call(
        functools.partial(_ar_kernel, dims),
        out_shape=jax.ShapeDtypeStruct((N, M), jnp.float32),
        in_specs=[pl.BlockSpec(memory_space=vmem)],
        out_specs=pl.BlockSpec(memory_space=vmem),
        scratch_shapes=[
            vmem((S1, M), jnp.float32),
            vmem((Y, S2, M), jnp.float32),
            vmem((X, S3, M), jnp.float32),
            vmem((S4, M), jnp.float32),
            vmem((ZH, S4, M), jnp.float32),
            vmem((S1, M), jnp.float32),
            vmem((S2, M), jnp.float32),
            vmem((S3, M), jnp.float32),
            vmem((S4, M), jnp.float32),
            vmem((N, M), jnp.float32),
            pltpu.SemaphoreType.DMA((nsem,)),
            pltpu.SemaphoreType.DMA((nsem,)),
        ],
        compiler_params=pltpu.CompilerParams(collective_id=0, has_side_effects=True),
    )(g)


def extended(x, sides, width):
    for axis, dim in sides:
        devices, length = (lax.axis_size(axis), x.shape[dim])
        up = [(i, (i + 1) % devices) for i in range(devices - 1)]
        down = [(j, i) for i, j in up]
        last = lax.slice_in_dim(x, length - width, length, axis=dim)
        first = lax.slice_in_dim(x, 0, width, axis=dim)
        before = lax.ppermute(last, axis, up)
        after = lax.ppermute(first, axis, down)
        x = jnp.concatenate([before, x, after], axis=dim)
    return x


def _dims():
    rows, blk = lax.axis_size("rows"), lax.axis_size("blk")
    return (2, rows // 4, 2, 2, blk // 2)


def local(cov_blocks, col_index, block_count, probes):
    rows_here, slots, block, _ = cov_blocks.shape
    tile_rows = probes.shape[0]
    probe_cols = probes.shape[1]
    zone_blocks = rows_here * lax.axis_size("blk")
    zone_number = lax.axis_index("rows")
    relative = col_index - (zone_number - 1) * zone_blocks
    window_blocks = 3 * zone_blocks
    inside = (relative >= 0) & (relative < window_blocks)
    slot_ids = lax.broadcasted_iota(jnp.int32, (rows_here, slots), 1)
    live_mask = inside & (slot_ids < block_count[:, None])
    column_ids = jnp.arange(window_blocks, dtype=jnp.int32)
    hits = (relative[:, :, None] == column_ids[None, None, :]) & live_mask[:, :, None]
    selector = hits.astype(jnp.bfloat16)
    window_matrix = jnp.einsum(
        "lsp,lsac->lapc", selector, cov_blocks, preferred_element_type=jnp.float32
    )
    window_matrix = window_matrix.astype(jnp.bfloat16).reshape(
        rows_here * block, window_blocks * block
    )

    def add_columns(running, shard_rows, first_row):
        length = shard_rows.shape[0]
        columns = lax.dynamic_slice_in_dim(window_matrix, first_row, length, 1)
        return running + jnp.dot(columns, shard_rows, preferred_element_type=jnp.float32)

    zeros_out = jnp.zeros((tile_rows, probe_cols), jnp.float32)
    own_zone = zone_gather(probes, lax.axis_size("blk"))
    zone_length = own_zone.shape[0]
    images = add_columns(zeros_out, own_zone, zone_length)
    near_zones = extended(own_zone, (("rows", 0),), zone_length)
    images = add_columns(images, lax.slice_in_dim(near_zones, 0, zone_length, axis=0), 0)
    images = add_columns(
        images,
        lax.slice_in_dim(near_zones, 2 * zone_length, 3 * zone_length, axis=0),
        2 * zone_length,
    )
    gram_local = lax.dot_general(
        images,
        images,
        (((0,), (0,)), ((), ())),
        precision=lax.Precision.HIGHEST,
        preferred_element_type=jnp.float32,
    )
    gram_total = gram_allreduce(gram_local, _dims())
    point_count = tile_rows * lax.axis_size("rows") * lax.axis_size("blk")
    gram_matrix = gram_total / point_count
    symmetric = (gram_matrix + gram_matrix.T) / 2
    factor_inverse = chol_inverse(symmetric)
    return _mm_t(images, factor_inverse)


def solution(mesh):
    return jax.shard_map(
        local,
        mesh=mesh,
        in_specs=(
            P(("rows", "blk"), None, None, None),
            P(("rows", "blk"), None),
            P(("rows", "blk")),
            P(("rows", "blk"), None),
        ),
        out_specs=P(("rows", "blk"), None),
        check_vma=False,
    )
```

profile of v0, /device:TPU:1, one launch (start us, length us, event | category | flops | bytes accessed | tf_op | source)
XLA Modules:
  0.0 209.2 jit_solution(2233059543689538557)
XLA Ops:
  0.0 0.0 copy-start
  0.0 32.1 %shard_map.46 = bf16[2048,512]{1,0:T(8,128)(2,1)} custom-call(bf16[256,512]{1,0:T(8,128)(2,1)} %p_ref.1), custom_call_target="tpu_custom_call" | custom-call | tf_op jit(solution)/shard_map/pallas_call | solution.py:177
  32.1 6.2 %collective-permute-start = (bf16[2048,512]{1,0:T(8,128)(2,1)}, bf16[2048,512]{1,0:T(8,128)(2,1)}, u32[]{:S(2)}, u32[]{:S(2)}) collective-permute-start(bf16[2048,512]{1,0:T(8,128)(2,1)} %shard_map.46), channel_id=1, source_target_pairs={{0,8},{8,16},{16,24},{24,32},{32,40},{40,48},{48,56},{56,64},{64,7... | collective-permute-start | bytes 6291464 | tf_op jit(solution)/shard_map/ppermute | solution.py:307
  38.4 1.9 collective-permute-start.1
  40.3 0.8 compare_and_fusion
  41.1 0.0 copy-done
  41.1 2.7 %fusion.2 = bf16[2,48,128,128]{3,1,2,0:T(8,128)(2,1)S(1)} fusion(bf16[2,40,128,128]{3,2,1,0:T(8,128)(2,1)S(1)} %copy-done, s32[2,40]{1,0:T(2,128)S(1)} %get-tuple-element.6, pred[2,40]{1,0:T(4,128)(4,1)S(1)} %get-tuple-element.5), kind=kOutput, calls=%fused_computation.3 | convolution fusion | flops 127409664 | bytes 5767568 | tf_op jit(solution)/shard_map/lsp,lsac->lapc/dot_general | solution.py:332
  43.8 0.0 copy-start.1
  43.8 0.8 copy.15
  44.6 0.8 copy-done.1
  45.3 0.7 fusion.7
  46.1 15.6 %collective-permute-done = bf16[2048,512]{1,0:T(8,128)(2,1)} collective-permute-done((bf16[2048,512]{1,0:T(8,128)(2,1)}, bf16[2048,512]{1,0:T(8,128)(2,1)}, u32[]{:S(2)}, u32[]{:S(2)}) %collective-permute-start) | collective-permute-done | bytes 2097184 | tf_op jit(solution)/shard_map/ppermute | solution.py:307
  61.6 2.3 %convolution_add_fusion.1 = f32[256,512]{1,0:T(8,128)S(1)} fusion(f32[256,512]{1,0:T(8,128)S(1)} %fusion.7, bf16[2048,512]{1,0:T(8,128)(2,1)} %collective-permute-done, bf16[256,6144]{1,0:T(8,128)(2,1)S(1)} %bitcast.24), kind=kOutput, calls=%fused_computation.5 | convolution fusion | flops 537001984 | bytes 4194304 | tf_op jit(solution)/shard_map/dot_general | solution.py:342
  63.9 2.1 %collective-permute-done.1 = bf16[2048,512]{1,0:T(8,128)(2,1)} collective-permute-done((bf16[2048,512]{1,0:T(8,128)(2,1)}, bf16[2048,512]{1,0:T(8,128)(2,1)}, u32[]{:S(2)}, u32[]{:S(2)}) %collective-permute-start.1) | collective-permute-done | bytes 2097184 | tf_op jit(solution)/shard_map/ppermute | solution.py:308
  66.0 2.3 %convolution_add_fusion = f32[256,512]{1,0:T(8,128)S(1)} fusion(f32[256,512]{1,0:T(8,128)S(1)} %convolution_add_fusion.1, bf16[2048,512]{1,0:T(8,128)(2,1)} %collective-permute-done.1, bf16[256,6144]{1,0:T(8,128)(2,1)S(1)} %bitcast.25), kind=kOutput, calls=%fused_computation.4 | convolution fusion | flops 537001984 | bytes 4194304 | tf_op jit(solution)/shard_map/dot_general | solution.py:342
  68.3 2.0 fusion.15.g_ref
  70.3 58.8 %shard_map.47 = f32[512,512]{1,0:T(8,128)} custom-call(f32[512,512]{1,0:T(8,128)} %fusion.15.g_ref), custom_call_target="tpu_custom_call" | custom-call | tf_op jit(solution)/shard_map/pallas_call | solution.py:277
  129.1 2.5 %copy.6 = f32[512,512]{0,1:T(8,128)} copy(f32[512,512]{1,0:T(8,128)} %shard_map.47) | data formatting | bytes 2097152 | tf_op jit(solution)/shard_map/pallas_call | solution.py:277
  131.7 2.3 %broadcast_multiply_fusion = f32[512,512]{0,1:T(8,128)} fusion(f32[512,512]{0,1:T(8,128)} %copy.6), kind=kLoop, calls=%fused_computation.12 | loop fusion | flops 262144 | bytes 2097152 | tf_op jit(solution)/shard_map/div | solution.py:364
  134.0 2.6 %copy.7 = f32[512,512]{1,0:T(8,128)} copy(f32[512,512]{0,1:T(8,128)} %broadcast_multiply_fusion) | data formatting | bytes 2097152 | tf_op jit(solution)/shard_map/div | solution.py:364
  136.5 2.8 %fusion.9.g_ref = f32[512,512]{1,0:T(8,128)} fusion(f32[512,512]{1,0:T(8,128)} %copy.7, f32[512,512]{0,1:T(8,128)} %copy.6), kind=kLoop, calls=%fused_computation.11 | loop fusion | flops 786432 | bytes 3145728 | tf_op jit(solution)/shard_map/div | solution.py:365
  139.3 66.8 %shard_map.48 = f32[512,512]{1,0:T(8,128)} custom-call(f32[512,512]{1,0:T(8,128)} %fusion.9.g_ref), custom_call_target="tpu_custom_call" | custom-call | tf_op jit(solution)/shard_map/pallas_call | solution.py:252
  206.1 3.1 %fusion.16 = f32[256,512]{1,0:T(8,128)} fusion(f32[256,512]{1,0:T(8,128)S(1)} %convolution_add_fusion, f32[512,512]{1,0:T(8,128)} %shard_map.48), kind=kOutput, calls=%fused_computation.21 | convolution fusion | flops 805306368 | bytes 2097152 | tf_op jit(solution)/shard_map/dot_general | solution.py:199
Async XLA Ops:
  0.0 41.1 %copy-start = (bf16[2,40,128,128]{3,2,1,0:T(8,128)(2,1)S(1)}, bf16[2,40,128,128]{3,2,1,0:T(8,128)(2,1)}, u32[]{:S(2)}) copy-start(bf16[2,40,128,128]{3,2,1,0:T(8,128)(2,1)} %param.4) | copy-start | bytes 7864324
  32.1 29.5 %collective-permute-start = (bf16[2048,512]{1,0:T(8,128)(2,1)}, bf16[2048,512]{1,0:T(8,128)(2,1)}, u32[]{:S(2)}, u32[]{:S(2)}) collective-permute-start(bf16[2048,512]{1,0:T(8,128)(2,1)} %shard_map.46), channel_id=1, source_target_pairs={{0,8},{8,16},{16,24},{24,32},{32,40},{40,48},{48,56},{56,64},{64,7... | collective-permute-start | bytes 6291464 | tf_op jit(solution)/shard_map/ppermute | solution.py:307
  38.4 27.7 %collective-permute-start.1 = (bf16[2048,512]{1,0:T(8,128)(2,1)}, bf16[2048,512]{1,0:T(8,128)(2,1)}, u32[]{:S(2)}, u32[]{:S(2)}) collective-permute-start(bf16[2048,512]{1,0:T(8,128)(2,1)} %shard_map.46), channel_id=1, source_target_pairs={{8,0},{16,8},{24,16},{32,24},{40,32},{48,40},{56,48},{64,56},{72,6... | collective-permute-start | bytes 6291464 | tf_op jit(solution)/shard_map/ppermute | solution.py:308
  43.8 1.6 copy-start.1
where the time goes:
time: 210 us; the launch traced here: 209 us
  Pallas kernels  158 us (75%)
  waiting for transfers between devices  17.7 us (8%)
  matrix products  13 us (6%)
  starting transfers between devices  8.16 us (4%)
  local copies, waits for them, and re-layouts  6.66 us (3%)
  other arithmetic  5.86 us (3%)
    pallas_call x1, Pallas kernels, chol_inverse(): pl.pallas_call(_chol_inv_kernel, out_shape=jax.ShapeDtypeStruct((n, n), j...  66.8 us
    pallas_call x1, Pallas kernels, gram_allreduce(): pl.pallas_call(functools.partial(_ar_kernel, dims), out_shape=jax.ShapeDt...  58.8 us
    pallas_call x1, Pallas kernels, zone_gather(): pl.pallas_call(functools.partial(_zone_gather_kernel, nb), out_shape=jax....  32.1 us
    ppermute x1, waiting for transfers between devices, extended(): before = lax.ppermute(last, axis, up)  15.6 us
    ppermute x1, starting transfers between devices, extended(): before = lax.ppermute(last, axis, up)  6.24 us
    dot_general x3, matrix products, add_columns(): jnp.dot(columns, shard_rows, preferred_element_type=jnp.float32)  5.28 us
  transfers between devices with their start and end apart: 2, of which 2 were waited for; matrix products, arithmetic and copies ran while one was open for 3% of the time, Pallas kernels for 0%

commit v1 on v0

--- a/solution.py
+++ b/solution.py
@@ -199,11 +199,12 @@
     return lax.dot_general(a, b, (((1,), (1,)), ((), ())), precision=HI, preferred_element_type=jnp.float32)
 
 
-def _chol_inv_kernel(g_ref, m_ref, a_ref, d_ref, b_ref, l_ref):
+def _chol_inv_kernel(count, g_ref, m_ref, a_ref, d_ref, b_ref, l_ref):
     n = g_ref.shape[0]
     t = d_ref.shape[0]
     nb = n // t
-    a_ref[...] = g_ref[...]
+    gram = g_ref[...] / count
+    a_ref[...] = (gram + gram.T) / 2
     m_ref[...] = jnp.zeros_like(m_ref)
     lane = lax.broadcasted_iota(jnp.int32, (1, t), 1)
     lane2 = lax.broadcasted_iota(jnp.int32, (t, t), 1)
@@ -229,7 +230,7 @@
         lo = k * t
         d_ref[...] = a_ref[lo:lo + t, lo:lo + t]
         b_ref[...] = eye
-        lax.fori_loop(0, t, step, 0)
+        lax.fori_loop(0, t, step, 0, unroll=4)
         m_ref[lo:lo + t, lo:lo + t] = b_ref[...]
         if k < nb - 1:
             hi = lo + t
@@ -246,11 +247,11 @@
             m_ref[i * t:(i + 1) * t, j * t:(j + 1) * t] = -_mm(m_ref[i * t:(i + 1) * t, i * t:(i + 1) * t], acc)
 
 
-def chol_inverse(g, t=128):
+def chol_inverse(g, count, t=128):
     n = g.shape[0]
     vmem = pltpu.VMEM
     return pl.pallas_call(
-        _chol_inv_kernel,
+        functools.partial(_chol_inv_kernel, count),
         out_shape=jax.ShapeDtypeStruct((n, n), jnp.float32),
         in_specs=[pl.BlockSpec(memory_space=vmem)],
         out_specs=pl.BlockSpec(memory_space=vmem),
@@ -361,9 +362,7 @@
     )
     gram_total = gram_allreduce(gram_local, _dims())
     point_count = tile_rows * lax.axis_size("rows") * lax.axis_size("blk")
-    gram_matrix = gram_total / point_count
-    symmetric = (gram_matrix + gram_matrix.T) / 2
-    factor_inverse = chol_inverse(symmetric)
+    factor_inverse = chol_inverse(gram_total, float(point_count))
     return _mm_t(images, factor_inverse)
 
 

time: 210 us -> 199 us (0.948)
  other arithmetic: 5.86 us -> 0.77 us
  local copies, waits for them, and re-layouts: 6.66 us -> 1.58 us
    div x2 -> x0, other arithmetic: 5.09 us -> none  [the longest x1 2.76 us: local(): symmetric = (gram_matrix + gram_matrix.T) / 2]
    div x1 -> x0, local copies, waits for them, and re-layouts: 2.55 us -> none  [local(): gram_matrix = gram_total / point_count]
    pallas_call x1 -> x0, local copies, waits for them, and re-layouts: 2.53 us -> none  [gram_allreduce(): pl.pallas_call(functools.partial(_ar_kernel, dims), out_shape=jax.ShapeDt...]
  transfers between devices with their start and end apart: 2 -> 2, of which waited for: 2 -> 2; matrix products, arithmetic and copies ran while one was open for 3% -> 4% of each run, Pallas kernels for 0% -> 0%
where the time goes in v1:
time: 199 us
  Pallas kernels  157 us (79%)
  waiting for transfers between devices  17.7 us (9%)
  matrix products  13.1 us (7%)
  starting transfers between devices  8.16 us (4%)
    pallas_call x1, Pallas kernels, chol_inverse(): pl.pallas_call(functools.partial(_chol_inv_kernel, count), out_shape=jax....  66.5 us
    pallas_call x1, Pallas kernels, gram_allreduce(): pl.pallas_call(functools.partial(_ar_kernel, dims), out_shape=jax.ShapeDt...  58.7 us
    pallas_call x1, Pallas kernels, zone_gather(): pl.pallas_call(functools.partial(_zone_gather_kernel, nb), out_shape=jax....  32.1 us
    ppermute x1, waiting for transfers between devices, extended(): before = lax.ppermute(last, axis, up)  15.6 us
    ppermute x1, starting transfers between devices, extended(): before = lax.ppermute(last, axis, up)  6.24 us
    dot_general x3, matrix products, add_columns(): jnp.dot(columns, shard_rows, preferred_element_type=jnp.float32)  5.28 us
  transfers between devices with their start and end apart: 2, of which 2 were waited for; matrix products, arithmetic and copies ran while one was open for 4% of the time, Pallas kernels for 0%

profile of v1, /device:TPU:1, one launch (start us, length us, event | category | flops | bytes accessed | tf_op | source)
XLA Modules:
  0.0 198.7 jit_solution(14443225911912027835)
XLA Ops:
  0.0 0.0 copy-start
  0.0 32.1 %shard_map.46 = bf16[2048,512]{1,0:T(8,128)(2,1)} custom-call(bf16[256,512]{1,0:T(8,128)(2,1)} %p_ref.1), custom_call_target="tpu_custom_call" | custom-call | tf_op jit(solution)/shard_map/pallas_call | solution.py:177
  32.1 6.2 %collective-permute-start = (bf16[2048,512]{1,0:T(8,128)(2,1)}, bf16[2048,512]{1,0:T(8,128)(2,1)}, u32[]{:S(2)}, u32[]{:S(2)}) collective-permute-start(bf16[2048,512]{1,0:T(8,128)(2,1)} %shard_map.46), channel_id=1, source_target_pairs={{0,8},{8,16},{16,24},{24,32},{32,40},{40,48},{48,56},{56,64},{64,7... | collective-permute-start | bytes 6291464 | tf_op jit(solution)/shard_map/ppermute | solution.py:308
  38.4 1.9 collective-permute-start.1
  40.3 0.8 compare_and_fusion
  41.1 0.0 copy-done
  41.1 2.7 %fusion.2 = bf16[2,48,128,128]{3,1,2,0:T(8,128)(2,1)S(1)} fusion(bf16[2,40,128,128]{3,2,1,0:T(8,128)(2,1)S(1)} %copy-done, s32[2,40]{1,0:T(2,128)S(1)} %get-tuple-element.6, pred[2,40]{1,0:T(4,128)(4,1)S(1)} %get-tuple-element.5), kind=kOutput, calls=%fused_computation.3 | convolution fusion | flops 127409664 | bytes 5767568 | tf_op jit(solution)/shard_map/lsp,lsac->lapc/dot_general | solution.py:333
  43.8 0.0 copy-start.1
  43.8 0.8 copy.13
  44.6 0.8 copy-done.1
  45.3 0.7 fusion.7
  46.1 15.6 %collective-permute-done = bf16[2048,512]{1,0:T(8,128)(2,1)} collective-permute-done((bf16[2048,512]{1,0:T(8,128)(2,1)}, bf16[2048,512]{1,0:T(8,128)(2,1)}, u32[]{:S(2)}, u32[]{:S(2)}) %collective-permute-start) | collective-permute-done | bytes 2097184 | tf_op jit(solution)/shard_map/ppermute | solution.py:308
  61.6 2.3 %convolution_add_fusion.1 = f32[256,512]{1,0:T(8,128)S(1)} fusion(f32[256,512]{1,0:T(8,128)S(1)} %fusion.7, bf16[2048,512]{1,0:T(8,128)(2,1)} %collective-permute-done, bf16[256,6144]{1,0:T(8,128)(2,1)S(1)} %bitcast.20), kind=kOutput, calls=%fused_computation.5 | convolution fusion | flops 537001984 | bytes 4194304 | tf_op jit(solution)/shard_map/dot_general | solution.py:343
  63.9 2.1 %collective-permute-done.1 = bf16[2048,512]{1,0:T(8,128)(2,1)} collective-permute-done((bf16[2048,512]{1,0:T(8,128)(2,1)}, bf16[2048,512]{1,0:T(8,128)(2,1)}, u32[]{:S(2)}, u32[]{:S(2)}) %collective-permute-start.1) | collective-permute-done | bytes 2097184 | tf_op jit(solution)/shard_map/ppermute | solution.py:309
  66.0 2.3 %convolution_add_fusion = f32[256,512]{1,0:T(8,128)S(1)} fusion(f32[256,512]{1,0:T(8,128)S(1)} %convolution_add_fusion.1, bf16[2048,512]{1,0:T(8,128)(2,1)} %collective-permute-done.1, bf16[256,6144]{1,0:T(8,128)(2,1)S(1)} %bitcast.21), kind=kOutput, calls=%fused_computation.4 | convolution fusion | flops 537001984 | bytes 4194304 | tf_op jit(solution)/shard_map/dot_general | solution.py:343
  68.3 2.1 %fusion.14.g_ref = f32[512,512]{1,0:T(8,128)} fusion(f32[256,512]{1,0:T(8,128)S(1)} %convolution_add_fusion), kind=kOutput, calls=%fused_computation.17 | convolution fusion | flops 805306368 | bytes 1572864 | tf_op jit(solution)/shard_map/dot_general | solution.py:356
  70.4 58.7 %shard_map.47.g_ref = f32[512,512]{1,0:T(8,128)} custom-call(f32[512,512]{1,0:T(8,128)} %fusion.14.g_ref), custom_call_target="tpu_custom_call" | custom-call | tf_op jit(solution)/shard_map/pallas_call | solution.py:278
  129.1 66.5 %shard_map.48 = f32[512,512]{1,0:T(8,128)} custom-call(f32[512,512]{1,0:T(8,128)} %shard_map.47.g_ref), custom_call_target="tpu_custom_call" | custom-call | tf_op jit(solution)/shard_map/pallas_call | solution.py:253
  195.7 3.1 %fusion.15 = f32[256,512]{1,0:T(8,128)} fusion(f32[256,512]{1,0:T(8,128)S(1)} %convolution_add_fusion, f32[512,512]{1,0:T(8,128)} %shard_map.48), kind=kOutput, calls=%fused_computation.18 | convolution fusion | flops 805306368 | bytes 2097152 | tf_op jit(solution)/shard_map/dot_general | solution.py:199
Async XLA Ops:
  0.0 41.1 %copy-start = (bf16[2,40,128,128]{3,2,1,0:T(8,128)(2,1)S(1)}, bf16[2,40,128,128]{3,2,1,0:T(8,128)(2,1)}, u32[]{:S(2)}) copy-start(bf16[2,40,128,128]{3,2,1,0:T(8,128)(2,1)} %param.4) | copy-start | bytes 7864324
  32.1 29.5 %collective-permute-start = (bf16[2048,512]{1,0:T(8,128)(2,1)}, bf16[2048,512]{1,0:T(8,128)(2,1)}, u32[]{:S(2)}, u32[]{:S(2)}) collective-permute-start(bf16[2048,512]{1,0:T(8,128)(2,1)} %shard_map.46), channel_id=1, source_target_pairs={{0,8},{8,16},{16,24},{24,32},{32,40},{40,48},{48,56},{56,64},{64,7... | collective-permute-start | bytes 6291464 | tf_op jit(solution)/shard_map/ppermute | solution.py:308
  38.4 27.7 %collective-permute-start.1 = (bf16[2048,512]{1,0:T(8,128)(2,1)}, bf16[2048,512]{1,0:T(8,128)(2,1)}, u32[]{:S(2)}, u32[]{:S(2)}) collective-permute-start(bf16[2048,512]{1,0:T(8,128)(2,1)} %shard_map.46), channel_id=1, source_target_pairs={{8,0},{16,8},{24,16},{32,24},{40,32},{48,40},{56,48},{64,56},{72,6... | collective-permute-start | bytes 6291464 | tf_op jit(solution)/shard_map/ppermute | solution.py:309
  43.8 1.6 copy-start.1

commit v2 on v1

--- a/solution.py
+++ b/solution.py
@@ -207,22 +207,22 @@
     a_ref[...] = (gram + gram.T) / 2
     m_ref[...] = jnp.zeros_like(m_ref)
     lane = lax.broadcasted_iota(jnp.int32, (1, t), 1)
-    lane2 = lax.broadcasted_iota(jnp.int32, (t, t), 1)
-    sub = lax.broadcasted_iota(jnp.int32, (t, 1), 0)
-    eye = (lax.broadcasted_iota(jnp.int32, (t, t), 0) == lane2).astype(jnp.float32)
-
-    def step(j, carry):
+    eye = (lax.broadcasted_iota(jnp.int32, (t, t), 0) == lax.broadcasted_iota(jnp.int32, (t, t), 1)).astype(jnp.float32)
+
+    def step(r0, j, carry):
+        lane2 = lax.broadcasted_iota(jnp.int32, (t - r0, t), 1)
+        sub = lax.broadcasted_iota(jnp.int32, (t - r0, 1), 0) + r0
         row = d_ref[pl.ds(j, 1), :]
         piv2 = jnp.sum(jnp.where(lane == j, row, 0.0), axis=1, keepdims=True)
         inv = 1.0 / jnp.sqrt(piv2)
-        dmat = d_ref[...]
+        dmat = d_ref[r0:, :]
         colfull = jnp.sum(jnp.where(lane2 == j, dmat, 0.0), axis=1, keepdims=True)
         col = jnp.where(sub >= j, colfull * inv, 0.0)
         lrow = jnp.where(lane >= j, row * inv, 0.0)
-        d_ref[...] = dmat - col * lrow
+        d_ref[r0:, :] = dmat - col * lrow
         brow = b_ref[pl.ds(j, 1), :] * inv
-        bmat = b_ref[...]
-        b_ref[...] = bmat - jnp.where(sub > j, col, 0.0) * brow
+        bmat = b_ref[r0:, :]
+        b_ref[r0:, :] = bmat - jnp.where(sub > j, col, 0.0) * brow
         b_ref[pl.ds(j, 1), :] = brow
         return carry
 
@@ -230,7 +230,8 @@
         lo = k * t
         d_ref[...] = a_ref[lo:lo + t, lo:lo + t]
         b_ref[...] = eye
-        lax.fori_loop(0, t, step, 0, unroll=4)
+        for r0 in range(0, t, 8):
+            lax.fori_loop(r0, r0 + 8, functools.partial(step, r0), 0)
         m_ref[lo:lo + t, lo:lo + t] = b_ref[...]
         if k < nb - 1:
             hi = lo + t

time: 199 us -> 194 us (0.975)
  Pallas kernels: 157 us -> 153 us
    pallas_call x1, Pallas kernels: 66.5 us -> 61.8 us  [chol_inverse(): pl.pallas_call(functools.partial(_chol_inv_kernel, count), out_shape=jax....]
where the time goes in v2:
time: 194 us
  Pallas kernels  153 us (79%)
  waiting for transfers between devices  17.7 us (9%)
  matrix products  13.1 us (7%)
  starting transfers between devices  8.16 us (4%)
    pallas_call x1, Pallas kernels, chol_inverse(): pl.pallas_call(functools.partial(_chol_inv_kernel, count), out_shape=jax....  61.8 us
    pallas_call x1, Pallas kernels, gram_allreduce(): pl.pallas_call(functools.partial(_ar_kernel, dims), out_shape=jax.ShapeDt...  58.7 us
    pallas_call x1, Pallas kernels, zone_gather(): pl.pallas_call(functools.partial(_zone_gather_kernel, nb), out_shape=jax....  32.1 us
    ppermute x1, waiting for transfers between devices, extended(): before = lax.ppermute(last, axis, up)  15.6 us
    ppermute x1, starting transfers between devices, extended(): before = lax.ppermute(last, axis, up)  6.24 us
    dot_general x3, matrix products, add_columns(): jnp.dot(columns, shard_rows, preferred_element_type=jnp.float32)  5.28 us
  transfers between devices with their start and end apart: 2, of which 2 were waited for; matrix products, arithmetic and copies ran while one was open for 4% of the time, Pallas kernels for 0%

profile of v2, /device:TPU:1, one launch (start us, length us, event | category | flops | bytes accessed | tf_op | source)
XLA Modules:
  0.0 194.1 jit_solution(3212979821224954411)
XLA Ops:
  0.0 0.0 copy-start
  0.0 32.1 %shard_map.46 = bf16[2048,512]{1,0:T(8,128)(2,1)} custom-call(bf16[256,512]{1,0:T(8,128)(2,1)} %p_ref.1), custom_call_target="tpu_custom_call" | custom-call | tf_op jit(solution)/shard_map/pallas_call | solution.py:177
  32.1 6.2 %collective-permute-start = (bf16[2048,512]{1,0:T(8,128)(2,1)}, bf16[2048,512]{1,0:T(8,128)(2,1)}, u32[]{:S(2)}, u32[]{:S(2)}) collective-permute-start(bf16[2048,512]{1,0:T(8,128)(2,1)} %shard_map.46), channel_id=1, source_target_pairs={{0,8},{8,16},{16,24},{24,32},{32,40},{40,48},{48,56},{56,64},{64,7... | collective-permute-start | bytes 6291464 | tf_op jit(solution)/shard_map/ppermute | solution.py:309
  38.4 1.9 collective-permute-start.1
  40.3 0.8 compare_and_fusion
  41.1 0.0 copy-done
  41.1 2.7 %fusion.2 = bf16[2,48,128,128]{3,1,2,0:T(8,128)(2,1)S(1)} fusion(bf16[2,40,128,128]{3,2,1,0:T(8,128)(2,1)S(1)} %copy-done, s32[2,40]{1,0:T(2,128)S(1)} %get-tuple-element.6, pred[2,40]{1,0:T(4,128)(4,1)S(1)} %get-tuple-element.5), kind=kOutput, calls=%fused_computation.3 | convolution fusion | flops 127409664 | bytes 5767568 | tf_op jit(solution)/shard_map/lsp,lsac->lapc/dot_general | solution.py:334
  43.8 0.0 copy-start.1
  43.8 0.8 copy.13
  44.6 0.8 copy-done.1
  45.3 0.7 fusion.7
  46.0 15.6 %collective-permute-done = bf16[2048,512]{1,0:T(8,128)(2,1)} collective-permute-done((bf16[2048,512]{1,0:T(8,128)(2,1)}, bf16[2048,512]{1,0:T(8,128)(2,1)}, u32[]{:S(2)}, u32[]{:S(2)}) %collective-permute-start) | collective-permute-done | bytes 2097184 | tf_op jit(solution)/shard_map/ppermute | solution.py:309
  61.6 2.3 %convolution_add_fusion.1 = f32[256,512]{1,0:T(8,128)S(1)} fusion(f32[256,512]{1,0:T(8,128)S(1)} %fusion.7, bf16[2048,512]{1,0:T(8,128)(2,1)} %collective-permute-done, bf16[256,6144]{1,0:T(8,128)(2,1)S(1)} %bitcast.20), kind=kOutput, calls=%fused_computation.5 | convolution fusion | flops 537001984 | bytes 4194304 | tf_op jit(solution)/shard_map/dot_general | solution.py:344
  63.9 2.1 %collective-permute-done.1 = bf16[2048,512]{1,0:T(8,128)(2,1)} collective-permute-done((bf16[2048,512]{1,0:T(8,128)(2,1)}, bf16[2048,512]{1,0:T(8,128)(2,1)}, u32[]{:S(2)}, u32[]{:S(2)}) %collective-permute-start.1) | collective-permute-done | bytes 2097184 | tf_op jit(solution)/shard_map/ppermute | solution.py:310
  66.0 2.3 %convolution_add_fusion = f32[256,512]{1,0:T(8,128)S(1)} fusion(f32[256,512]{1,0:T(8,128)S(1)} %convolution_add_fusion.1, bf16[2048,512]{1,0:T(8,128)(2,1)} %collective-permute-done.1, bf16[256,6144]{1,0:T(8,128)(2,1)S(1)} %bitcast.21), kind=kOutput, calls=%fused_computation.4 | convolution fusion | flops 537001984 | bytes 4194304 | tf_op jit(solution)/shard_map/dot_general | solution.py:344
  68.3 2.1 %fusion.14.g_ref = f32[512,512]{1,0:T(8,128)} fusion(f32[256,512]{1,0:T(8,128)S(1)} %convolution_add_fusion), kind=kOutput, calls=%fused_computation.17 | convolution fusion | flops 805306368 | bytes 1572864 | tf_op jit(solution)/shard_map/dot_general | solution.py:357
  70.4 58.7 %shard_map.47.g_ref = f32[512,512]{1,0:T(8,128)} custom-call(f32[512,512]{1,0:T(8,128)} %fusion.14.g_ref), custom_call_target="tpu_custom_call" | custom-call | tf_op jit(solution)/shard_map/pallas_call | solution.py:279
  129.1 61.8 %shard_map.48 = f32[512,512]{1,0:T(8,128)} custom-call(f32[512,512]{1,0:T(8,128)} %shard_map.47.g_ref), custom_call_target="tpu_custom_call" | custom-call | tf_op jit(solution)/shard_map/pallas_call | solution.py:254
  191.0 3.1 %fusion.15 = f32[256,512]{1,0:T(8,128)} fusion(f32[256,512]{1,0:T(8,128)S(1)} %convolution_add_fusion, f32[512,512]{1,0:T(8,128)} %shard_map.48), kind=kOutput, calls=%fused_computation.18 | convolution fusion | flops 805306368 | bytes 2097152 | tf_op jit(solution)/shard_map/dot_general | solution.py:199
Async XLA Ops:
  0.0 41.1 %copy-start = (bf16[2,40,128,128]{3,2,1,0:T(8,128)(2,1)S(1)}, bf16[2,40,128,128]{3,2,1,0:T(8,128)(2,1)}, u32[]{:S(2)}) copy-start(bf16[2,40,128,128]{3,2,1,0:T(8,128)(2,1)} %param.4) | copy-start | bytes 7864324
  32.1 29.5 %collective-permute-start = (bf16[2048,512]{1,0:T(8,128)(2,1)}, bf16[2048,512]{1,0:T(8,128)(2,1)}, u32[]{:S(2)}, u32[]{:S(2)}) collective-permute-start(bf16[2048,512]{1,0:T(8,128)(2,1)} %shard_map.46), channel_id=1, source_target_pairs={{0,8},{8,16},{16,24},{24,32},{32,40},{40,48},{48,56},{56,64},{64,7... | collective-permute-start | bytes 6291464 | tf_op jit(solution)/shard_map/ppermute | solution.py:309
  38.4 27.7 %collective-permute-start.1 = (bf16[2048,512]{1,0:T(8,128)(2,1)}, bf16[2048,512]{1,0:T(8,128)(2,1)}, u32[]{:S(2)}, u32[]{:S(2)}) collective-permute-start(bf16[2048,512]{1,0:T(8,128)(2,1)} %shard_map.46), channel_id=1, source_target_pairs={{8,0},{16,8},{24,16},{32,24},{40,32},{48,40},{56,48},{64,56},{72,6... | collective-permute-start | bytes 6291464 | tf_op jit(solution)/shard_map/ppermute | solution.py:310
  43.8 1.6 copy-start.1

commit v3 on v2

--- a/solution.py
+++ b/solution.py
@@ -144,45 +144,99 @@
     out_ref[...] = full[...]
 
 
-def _zone_gather_kernel(nb, p_ref, out_ref, ssem, rsem, lsem):
+def _window_gather_kernel(nr, nb, p_ref, out_ref, zbuf, ssem, rsem, lsem):
     T = p_ref.shape[0]
     r = lax.axis_index("rows")
     b = lax.axis_index("blk")
+    has_up = r > 0
+    has_dn = r < nr - 1
     barrier = pltpu.get_barrier_semaphore()
     for k in range(1, nb):
         pl.semaphore_signal(barrier, inc=1, device_id=(r, (b + k) % nb), device_id_type=MESH_ID)
-    pl.semaphore_wait(barrier, nb - 1)
-    here = pl.ds(pl.multiple_of(b * T, 8), T)
-    ds = []
-    for k in range(1, nb):
-        d = pltpu.make_async_remote_copy(
-            src_ref=p_ref, dst_ref=out_ref.at[here], send_sem=ssem.at[k - 1], recv_sem=rsem.at[b],
-            device_id=(r, (b + k) % nb), device_id_type=MESH_ID)
-        d.start()
-        ds.append(d)
-    own = pltpu.make_async_copy(p_ref, out_ref.at[here], lsem.at[0])
+
+    @pl.when(has_up)
+    def _():
+        pl.semaphore_signal(barrier, inc=1, device_id=(r - 1, b), device_id_type=MESH_ID)
+
+    @pl.when(has_dn)
+    def _():
+        pl.semaphore_signal(barrier, inc=1, device_id=(r + 1, b), device_id_type=MESH_ID)
+
+    pl.semaphore_wait(barrier, nb - 1 + has_up.astype(jnp.int32) + has_dn.astype(jnp.int32))
+
+    def block(j):
+        return pl.ds(pl.multiple_of(j * T, 8), T)
+
+    def copy(src, slot, j, sidx, peer):
+        return pltpu.make_async_remote_copy(
+            src_ref=src, dst_ref=out_ref.at[slot, block(j)], send_sem=ssem.at[sidx],
+            recv_sem=rsem.at[slot * nb + j], device_id=peer, device_id_type=MESH_ID)
+
+    zone_peers = [(k, (b + k) % nb) for k in range(1, nb)]
+    for k, p in zone_peers:
+        copy(p_ref, 1, b, k - 1, (r, p)).start()
+    own = pltpu.make_async_copy(p_ref, out_ref.at[1, block(b)], lsem.at[0])
     own.start()
+
+    @pl.when(has_dn)
+    def _():
+        copy(p_ref, 0, b, nb - 1, (r + 1, b)).start()
+
+    @pl.when(has_up)
+    def _():
+        copy(p_ref, 2, b, nb, (r - 1, b)).start()
+
+    for slot, cond, src_row, base in ((0, has_up, r - 1, nb + 1), (2, has_dn, r + 1, 2 * nb)):
+        @pl.when(cond)
+        def _():
+            copy(out_ref.at[slot, block(b)], slot, b, 0, (src_row, b)).wait_recv()
+            for k, p in zone_peers:
+                copy(out_ref.at[slot, block(b)], slot, b, base + k - 1, (r, p)).start()
+
+        @pl.when(jnp.logical_not(cond))
+        def _():
+            zbuf[...] = jnp.zeros_like(zbuf)
+            fill = pltpu.make_async_copy(zbuf, out_ref.at[slot], lsem.at[1])
+            fill.start()
+            fill.wait()
+
     for k in range(1, nb):
         s = (b - k + nb) % nb
-        pltpu.make_async_remote_copy(
-            src_ref=p_ref, dst_ref=out_ref.at[pl.ds(pl.multiple_of(s * T, 8), T)], send_sem=ssem.at[0],
-            recv_sem=rsem.at[s], device_id=(r, s), device_id_type=MESH_ID).wait_recv()
-    for d in ds:
-        d.wait_send()
+        copy(p_ref, 1, s, 0, (r, s)).wait_recv()
+    for slot, cond, base in ((0, has_up, nb + 1), (2, has_dn, 2 * nb)):
+        @pl.when(cond)
+        def _():
+            for k in range(1, nb):
+                s = (b - k + nb) % nb
+                copy(p_ref, slot, s, 0, (r, s)).wait_recv()
+            for k, p in zone_peers:
+                copy(out_ref.at[slot, block(b)], slot, b, base + k - 1, (r, p)).wait_send()
+
+    for k, p in zone_peers:
+        copy(p_ref, 1, b, k - 1, (r, p)).wait_send()
     own.wait()
 
-
-def zone_gather(p, nb):
+    @pl.when(has_dn)
+    def _():
+        copy(p_ref, 0, b, nb - 1, (r + 1, b)).wait_send()
+
+    @pl.when(has_up)
+    def _():
+        copy(p_ref, 2, b, nb, (r - 1, b)).wait_send()
+
+
+def window_gather(p, nr, nb):
     T, K = p.shape
     return pl.pallas_call(
-        functools.partial(_zone_gather_kernel, nb),
-        out_shape=jax.ShapeDtypeStruct((nb * T, K), p.dtype),
+        functools.partial(_window_gather_kernel, nr, nb),
+        out_shape=jax.ShapeDtypeStruct((3, nb * T, K), p.dtype),
         in_specs=[pl.BlockSpec(memory_space=pl.ANY)],
         out_specs=pl.BlockSpec(memory_space=pl.ANY),
         scratch_shapes=[
-            pltpu.SemaphoreType.DMA((nb - 1,)),
-            pltpu.SemaphoreType.DMA((nb,)),
-            pltpu.SemaphoreType.DMA((1,)),
+            pltpu.VMEM((nb * T, K), p.dtype),
+            pltpu.SemaphoreType.DMA((3 * nb,)),
+            pltpu.SemaphoreType.DMA((3 * nb,)),
+            pltpu.SemaphoreType.DMA((2,)),
         ],
         compiler_params=pltpu.CompilerParams(collective_id=1, has_side_effects=True),
     )(p)
@@ -299,19 +353,6 @@
     )(g)
 
 
-def extended(x, sides, width):
-    for axis, dim in sides:
-        devices, length = (lax.axis_size(axis), x.shape[dim])
-        up = [(i, (i + 1) % devices) for i in range(devices - 1)]
-        down = [(j, i) for i, j in up]
-        last = lax.slice_in_dim(x, length - width, length, axis=dim)
-        first = lax.slice_in_dim(x, 0, width, axis=dim)
-        before = lax.ppermute(last, axis, up)
-        after = lax.ppermute(first, axis, down)
-        x = jnp.concatenate([before, x, after], axis=dim)
-    return x
-
-
 def _dims():
     rows, blk = lax.axis_size("rows"), lax.axis_size("blk")
     return (2, rows // 4, 2, 2, blk // 2)
@@ -338,21 +379,9 @@
         rows_here * block, window_blocks * block
     )
 
-    def add_columns(running, shard_rows, first_row):
-        length = shard_rows.shape[0]
-        columns = lax.dynamic_slice_in_dim(window_matrix, first_row, length, 1)
-        return running + jnp.dot(columns, shard_rows, preferred_element_type=jnp.float32)
-
-    zeros_out = jnp.zeros((tile_rows, probe_cols), jnp.float32)
-    own_zone = zone_gather(probes, lax.axis_size("blk"))
-    zone_length = own_zone.shape[0]
-    images = add_columns(zeros_out, own_zone, zone_length)
-    near_zones = extended(own_zone, (("rows", 0),), zone_length)
-    images = add_columns(images, lax.slice_in_dim(near_zones, 0, zone_length, axis=0), 0)
-    images = add_columns(
-        images,
-        lax.slice_in_dim(near_zones, 2 * zone_length, 3 * zone_length, axis=0),
-        2 * zone_length,
+    window = window_gather(probes, lax.axis_size("rows"), lax.axis_size("blk"))
+    images = jnp.dot(
+        window_matrix, window.reshape(window_blocks * block, probe_cols), preferred_element_type=jnp.float32
     )
     gram_local = lax.dot_general(
         images,

time: 194 us -> 229 us (1.18)
  Pallas kernels: 153 us -> 211 us
  waiting for transfers between devices: 17.7 us -> 0 us
  starting transfers between devices: 8.16 us -> 0 us
    pallas_call x1, Pallas kernels: 32.1 us -> 75.3 us  [window_gather(): pl.pallas_call(functools.partial(_window_gather_kernel, nr, nb), out_shap...]
    ppermute x2 -> x0, waiting for transfers between devices: 17.7 us -> none  [the longest x1 15.6 us: extended(): before = lax.ppermute(last, axis, up)]
    pallas_call x1, Pallas kernels: 58.7 us -> 74.5 us  [gram_allreduce(): pl.pallas_call(functools.partial(_ar_kernel, dims), out_shape=jax.ShapeDt...]
    ppermute x2 -> x0, starting transfers between devices: 8.16 us -> none  [the longest x1 6.24 us: extended(): before = lax.ppermute(last, axis, up)]
    dot_general x3 -> x1, matrix products: 5.28 us -> 5.54 us  [local(): jnp.dot(window_matrix, window.reshape(window_blocks * block, probe_cols),...]
  transfers between devices with their start and end apart: 2 -> 0, of which waited for: 2 -> 0; matrix products, arithmetic and copies ran while one was open for 4% -> 0% of each run, Pallas kernels for 0% -> 0%
where the time goes in v3:
time: 229 us; the launch traced here: 228 us
  Pallas kernels  211 us (92%)
  matrix products  15.1 us (7%)
    pallas_call x1, Pallas kernels, window_gather(): pl.pallas_call(functools.partial(_window_gather_kernel, nr, nb), out_shap...  75.3 us
    pallas_call x1, Pallas kernels, gram_allreduce(): pl.pallas_call(functools.partial(_ar_kernel, dims), out_shape=jax.ShapeDt...  74.5 us
    pallas_call x1, Pallas kernels, chol_inverse(): pl.pallas_call(functools.partial(_chol_inv_kernel, count), out_shape=jax....  61.7 us
    dot_general x1, matrix products, local(): jnp.dot(window_matrix, window.reshape(window_blocks * block, probe_cols),...  5.54 us

profile of v3, /device:TPU:1, one launch (start us, length us, event | category | flops | bytes accessed | tf_op | source)
XLA Modules:
  0.0 228.3 jit_solution(13657404472554865451)
XLA Ops:
  0.0 0.0 copy-start
  0.0 0.9 compare_and_fusion
  0.9 0.9 copy-done
  1.8 4.4 %fusion.5 = bf16[2,48,128,128]{3,1,2,0:T(8,128)(2,1)} fusion(bf16[2,40,128,128]{3,2,1,0:T(8,128)(2,1)S(1)} %copy-done, s32[2,40]{1,0:T(2,128)S(1)} %get-tuple-element.6, pred[2,40]{1,0:T(4,128)(4,1)S(1)} %get-tuple-element.5), kind=kOutput, calls=%fused_computation.5 | convolution fusion | flops 127409664 | bytes 5767568 | tf_op jit(solution)/shard_map/lsp,lsac->lapc/dot_general | solution.py:375
  6.1 75.3 %shard_map.46 = bf16[3,2048,512]{2,1,0:T(8,128)(2,1)} custom-call(bf16[256,512]{1,0:T(8,128)(2,1)} %p_ref.1), custom_call_target="tpu_custom_call" | custom-call | tf_op jit(solution)/shard_map/pallas_call | solution.py:230
  81.4 5.5 %fusion = f32[256,512]{1,0:T(8,128)S(1)} fusion(bf16[6144,512]{1,0:T(8,128)(2,1)} %bitcast.17, bf16[32,8,48,128]{3,2,1,0:T(8,128)(2,1)} %bitcast.18), kind=kOutput, calls=%fused_computation | convolution fusion | flops 1610612736 | bytes 9961472 | tf_op jit(solution)/shard_map/dot_general | solution.py:383
  87.0 2.1 fusion.13.g_ref
  89.0 74.5 %shard_map.47.g_ref = f32[512,512]{1,0:T(8,128)} custom-call(f32[512,512]{1,0:T(8,128)} %fusion.13.g_ref), custom_call_target="tpu_custom_call" | custom-call | tf_op jit(solution)/shard_map/pallas_call | solution.py:333
  163.6 61.7 %shard_map.48 = f32[512,512]{1,0:T(8,128)} custom-call(f32[512,512]{1,0:T(8,128)} %shard_map.47.g_ref), custom_call_target="tpu_custom_call" | custom-call | tf_op jit(solution)/shard_map/pallas_call | solution.py:308
  225.2 3.1 %fusion.14 = f32[256,512]{1,0:T(8,128)} fusion(f32[256,512]{1,0:T(8,128)S(1)} %fusion, f32[512,512]{1,0:T(8,128)} %shard_map.48), kind=kOutput, calls=%fused_computation.14 | convolution fusion | flops 805306368 | bytes 2097152 | tf_op jit(solution)/shard_map/dot_general | solution.py:253
Async XLA Ops:
  0.0 1.8 copy-start

commit v4 on v3

--- a/solution.py
+++ b/solution.py
@@ -172,26 +172,33 @@
             src_ref=src, dst_ref=out_ref.at[slot, block(j)], send_sem=ssem.at[sidx],
             recv_sem=rsem.at[slot * nb + j], device_id=peer, device_id_type=MESH_ID)
 
+    def to_neighbours(src, j, start):
+        @pl.when(has_dn)
+        def _():
+            d = copy(src, 0, j, nb - 1 + j, (r + 1, b))
+            d.start() if start else d.wait_send()
+
+        @pl.when(has_up)
+        def _():
+            d = copy(src, 2, j, 2 * nb - 1 + j, (r - 1, b))
+            d.start() if start else d.wait_send()
+
     zone_peers = [(k, (b + k) % nb) for k in range(1, nb)]
     for k, p in zone_peers:
         copy(p_ref, 1, b, k - 1, (r, p)).start()
+    to_neighbours(p_ref, b, True)
     own = pltpu.make_async_copy(p_ref, out_ref.at[1, block(b)], lsem.at[0])
     own.start()
-
-    @pl.when(has_dn)
-    def _():
-        copy(p_ref, 0, b, nb - 1, (r + 1, b)).start()
-
-    @pl.when(has_up)
-    def _():
-        copy(p_ref, 2, b, nb, (r - 1, b)).start()
-
-    for slot, cond, src_row, base in ((0, has_up, r - 1, nb + 1), (2, has_dn, r + 1, 2 * nb)):
+    for k in range(1, nb):
+        s = (b - k + nb) % nb
+        copy(p_ref, 1, s, 0, (r, s)).wait_recv()
+        to_neighbours(out_ref.at[1, block(s)], s, True)
+
+    for slot, cond, src_row in ((0, has_up, r - 1), (2, has_dn, r + 1)):
         @pl.when(cond)
         def _():
-            copy(out_ref.at[slot, block(b)], slot, b, 0, (src_row, b)).wait_recv()
-            for k, p in zone_peers:
-                copy(out_ref.at[slot, block(b)], slot, b, base + k - 1, (r, p)).start()
+            for j in range(nb):
+                copy(p_ref, slot, j, 0, (src_row, b)).wait_recv()
 
         @pl.when(jnp.logical_not(cond))
         def _():
@@ -200,29 +207,11 @@
             fill.start()
             fill.wait()
 
-    for k in range(1, nb):
-        s = (b - k + nb) % nb
-        copy(p_ref, 1, s, 0, (r, s)).wait_recv()
-    for slot, cond, base in ((0, has_up, nb + 1), (2, has_dn, 2 * nb)):
-        @pl.when(cond)
-        def _():
-            for k in range(1, nb):
-                s = (b - k + nb) % nb
-                copy(p_ref, slot, s, 0, (r, s)).wait_recv()
-            for k, p in zone_peers:
-                copy(out_ref.at[slot, block(b)], slot, b, base + k - 1, (r, p)).wait_send()
-
     for k, p in zone_peers:
         copy(p_ref, 1, b, k - 1, (r, p)).wait_send()
     own.wait()
-
-    @pl.when(has_dn)
-    def _():
-        copy(p_ref, 0, b, nb - 1, (r + 1, b)).wait_send()
-
-    @pl.when(has_up)
-    def _():
-        copy(p_ref, 2, b, nb, (r - 1, b)).wait_send()
+    for j in range(nb):
+        to_neighbours(p_ref, j, False)
 
 
 def window_gather(p, nr, nb):

time: 229 us -> 206 us (0.90)
  Pallas kernels: 211 us -> 189 us
    pallas_call x1, Pallas kernels: 75.3 us -> 53.7 us  [window_gather(): pl.pallas_call(functools.partial(_window_gather_kernel, nr, nb), out_shap...]
where the time goes in v4:
time: 206 us
  Pallas kernels  189 us (92%)
  matrix products  15 us (7%)
    pallas_call x1, Pallas kernels, gram_allreduce(): pl.pallas_call(functools.partial(_ar_kernel, dims), out_shape=jax.ShapeDt...  73.5 us
    pallas_call x1, Pallas kernels, chol_inverse(): pl.pallas_call(functools.partial(_chol_inv_kernel, count), out_shape=jax....  61.7 us
    pallas_call x1, Pallas kernels, window_gather(): pl.pallas_call(functools.partial(_window_gather_kernel, nr, nb), out_shap...  53.7 us
    dot_general x1, matrix products, local(): jnp.dot(window_matrix, window.reshape(window_blocks * block, probe_cols),...  5.53 us
    dot_general x1, matrix products, local(): jnp.einsum('lsp,lsac->lapc', selector, cov_blocks, preferred_element_type...  4.37 us

profile of v4, /device:TPU:1, one launch (start us, length us, event | category | flops | bytes accessed | tf_op | source)
XLA Modules:
  0.0 205.8 jit_solution(9596964471241916864)
XLA Ops:
  0.0 0.0 copy-start
  0.0 0.9 compare_and_fusion
  0.9 0.9 copy-done
  1.8 4.4 %fusion.5 = bf16[2,48,128,128]{3,1,2,0:T(8,128)(2,1)} fusion(bf16[2,40,128,128]{3,2,1,0:T(8,128)(2,1)S(1)} %copy-done, s32[2,40]{1,0:T(2,128)S(1)} %get-tuple-element.6, pred[2,40]{1,0:T(4,128)(4,1)S(1)} %get-tuple-element.5), kind=kOutput, calls=%fused_computation.5 | convolution fusion | flops 127409664 | bytes 5767568 | tf_op jit(solution)/shard_map/lsp,lsac->lapc/dot_general | solution.py:364
  6.1 53.7 %shard_map.46 = bf16[3,2048,512]{2,1,0:T(8,128)(2,1)} custom-call(bf16[256,512]{1,0:T(8,128)(2,1)} %p_ref.1), custom_call_target="tpu_custom_call" | custom-call | tf_op jit(solution)/shard_map/pallas_call | solution.py:219
  59.9 5.5 %fusion = f32[256,512]{1,0:T(8,128)S(1)} fusion(bf16[6144,512]{1,0:T(8,128)(2,1)} %bitcast.17, bf16[32,8,48,128]{3,2,1,0:T(8,128)(2,1)} %bitcast.18), kind=kOutput, calls=%fused_computation | convolution fusion | flops 1610612736 | bytes 9961472 | tf_op jit(solution)/shard_map/dot_general | solution.py:372
  65.4 2.1 %fusion.13.g_ref = f32[512,512]{1,0:T(8,128)} fusion(f32[256,512]{1,0:T(8,128)S(1)} %fusion), kind=kOutput, calls=%fused_computation.13 | convolution fusion | flops 805306368 | bytes 1572864 | tf_op jit(solution)/shard_map/dot_general | solution.py:375
  67.5 73.5 %shard_map.47.g_ref = f32[512,512]{1,0:T(8,128)} custom-call(f32[512,512]{1,0:T(8,128)} %fusion.13.g_ref), custom_call_target="tpu_custom_call" | custom-call | tf_op jit(solution)/shard_map/pallas_call | solution.py:322
  141.0 61.7 %shard_map.48 = f32[512,512]{1,0:T(8,128)} custom-call(f32[512,512]{1,0:T(8,128)} %shard_map.47.g_ref), custom_call_target="tpu_custom_call" | custom-call | tf_op jit(solution)/shard_map/pallas_call | solution.py:297
  202.7 3.1 %fusion.14 = f32[256,512]{1,0:T(8,128)} fusion(f32[256,512]{1,0:T(8,128)S(1)} %fusion, f32[512,512]{1,0:T(8,128)} %shard_map.48), kind=kOutput, calls=%fused_computation.14 | convolution fusion | flops 805306368 | bytes 2097152 | tf_op jit(solution)/shard_map/dot_general | solution.py:242
Async XLA Ops:
  0.0 1.8 copy-start

commit v5 on v2

--- a/solution.py
+++ b/solution.py
@@ -214,7 +214,7 @@
         sub = lax.broadcasted_iota(jnp.int32, (t - r0, 1), 0) + r0
         row = d_ref[pl.ds(j, 1), :]
         piv2 = jnp.sum(jnp.where(lane == j, row, 0.0), axis=1, keepdims=True)
-        inv = 1.0 / jnp.sqrt(piv2)
+        inv = lax.rsqrt(piv2)
         dmat = d_ref[r0:, :]
         colfull = jnp.sum(jnp.where(lane2 == j, dmat, 0.0), axis=1, keepdims=True)
         col = jnp.where(sub >= j, colfull * inv, 0.0)

time: 194 us -> 191 us (0.985)
  Pallas kernels: 153 us -> 149 us
    pallas_call x1, Pallas kernels: 61.8 us -> 58 us  [chol_inverse(): pl.pallas_call(functools.partial(_chol_inv_kernel, count), out_shape=jax....]
where the time goes in v5:
time: 191 us; the launch traced here: 190 us
  Pallas kernels  149 us (78%)
  waiting for transfers between devices  17.7 us (9%)
  matrix products  13.1 us (7%)
  starting transfers between devices  8.16 us (4%)
    pallas_call x1, Pallas kernels, gram_allreduce(): pl.pallas_call(functools.partial(_ar_kernel, dims), out_shape=jax.ShapeDt...  58.7 us
    pallas_call x1, Pallas kernels, chol_inverse(): pl.pallas_call(functools.partial(_chol_inv_kernel, count), out_shape=jax....  58 us
    pallas_call x1, Pallas kernels, zone_gather(): pl.pallas_call(functools.partial(_zone_gather_kernel, nb), out_shape=jax....  32.1 us
    ppermute x1, waiting for transfers between devices, extended(): before = lax.ppermute(last, axis, up)  15.6 us
    ppermute x1, starting transfers between devices, extended(): before = lax.ppermute(last, axis, up)  6.24 us
    dot_general x3, matrix products, add_columns(): jnp.dot(columns, shard_rows, preferred_element_type=jnp.float32)  5.28 us
  transfers between devices with their start and end apart: 2, of which 2 were waited for; matrix products, arithmetic and copies ran while one was open for 4% of the time, Pallas kernels for 0%

profile of v5, /device:TPU:1, one launch (start us, length us, event | category | flops | bytes accessed | tf_op | source)
XLA Modules:
  0.0 190.3 jit_solution(2500891289808131517)
XLA Ops:
  0.0 0.0 copy-start
  0.0 32.1 %shard_map.46 = bf16[2048,512]{1,0:T(8,128)(2,1)} custom-call(bf16[256,512]{1,0:T(8,128)(2,1)} %p_ref.1), custom_call_target="tpu_custom_call" | custom-call | tf_op jit(solution)/shard_map/pallas_call | solution.py:177
  32.1 6.2 %collective-permute-start = (bf16[2048,512]{1,0:T(8,128)(2,1)}, bf16[2048,512]{1,0:T(8,128)(2,1)}, u32[]{:S(2)}, u32[]{:S(2)}) collective-permute-start(bf16[2048,512]{1,0:T(8,128)(2,1)} %shard_map.46), channel_id=1, source_target_pairs={{0,8},{8,16},{16,24},{24,32},{32,40},{40,48},{48,56},{56,64},{64,7... | collective-permute-start | bytes 6291464 | tf_op jit(solution)/shard_map/ppermute | solution.py:309
  38.4 1.9 %collective-permute-start.1 = (bf16[2048,512]{1,0:T(8,128)(2,1)}, bf16[2048,512]{1,0:T(8,128)(2,1)}, u32[]{:S(2)}, u32[]{:S(2)}) collective-permute-start(bf16[2048,512]{1,0:T(8,128)(2,1)} %shard_map.46), channel_id=1, source_target_pairs={{8,0},{16,8},{24,16},{32,24},{40,32},{48,40},{56,48},{64,56},{72,6... | collective-permute-start | bytes 6291464 | tf_op jit(solution)/shard_map/ppermute | solution.py:310
  40.3 0.8 compare_and_fusion
  41.1 0.0 copy-done
  41.1 2.7 %fusion.2 = bf16[2,48,128,128]{3,1,2,0:T(8,128)(2,1)S(1)} fusion(bf16[2,40,128,128]{3,2,1,0:T(8,128)(2,1)S(1)} %copy-done, s32[2,40]{1,0:T(2,128)S(1)} %get-tuple-element.6, pred[2,40]{1,0:T(4,128)(4,1)S(1)} %get-tuple-element.5), kind=kOutput, calls=%fused_computation.3 | convolution fusion | flops 127409664 | bytes 5767568 | tf_op jit(solution)/shard_map/lsp,lsac->lapc/dot_general | solution.py:334
  43.8 0.0 copy-start.1
  43.8 0.8 copy.13
  44.6 0.8 copy-done.1
  45.3 0.7 fusion.7
  46.0 15.6 %collective-permute-done = bf16[2048,512]{1,0:T(8,128)(2,1)} collective-permute-done((bf16[2048,512]{1,0:T(8,128)(2,1)}, bf16[2048,512]{1,0:T(8,128)(2,1)}, u32[]{:S(2)}, u32[]{:S(2)}) %collective-permute-start) | collective-permute-done | bytes 2097184 | tf_op jit(solution)/shard_map/ppermute | solution.py:309
  61.6 2.3 %convolution_add_fusion.1 = f32[256,512]{1,0:T(8,128)S(1)} fusion(f32[256,512]{1,0:T(8,128)S(1)} %fusion.7, bf16[2048,512]{1,0:T(8,128)(2,1)} %collective-permute-done, bf16[256,6144]{1,0:T(8,128)(2,1)S(1)} %bitcast.20), kind=kOutput, calls=%fused_computation.5 | convolution fusion | flops 537001984 | bytes 4194304 | tf_op jit(solution)/shard_map/dot_general | solution.py:344
  63.9 2.1 %collective-permute-done.1 = bf16[2048,512]{1,0:T(8,128)(2,1)} collective-permute-done((bf16[2048,512]{1,0:T(8,128)(2,1)}, bf16[2048,512]{1,0:T(8,128)(2,1)}, u32[]{:S(2)}, u32[]{:S(2)}) %collective-permute-start.1) | collective-permute-done | bytes 2097184 | tf_op jit(solution)/shard_map/ppermute | solution.py:310
  66.0 2.3 %convolution_add_fusion = f32[256,512]{1,0:T(8,128)S(1)} fusion(f32[256,512]{1,0:T(8,128)S(1)} %convolution_add_fusion.1, bf16[2048,512]{1,0:T(8,128)(2,1)} %collective-permute-done.1, bf16[256,6144]{1,0:T(8,128)(2,1)S(1)} %bitcast.21), kind=kOutput, calls=%fused_computation.4 | convolution fusion | flops 537001984 | bytes 4194304 | tf_op jit(solution)/shard_map/dot_general | solution.py:344
  68.3 2.1 %fusion.14.g_ref = f32[512,512]{1,0:T(8,128)} fusion(f32[256,512]{1,0:T(8,128)S(1)} %convolution_add_fusion), kind=kOutput, calls=%fused_computation.17 | convolution fusion | flops 805306368 | bytes 1572864 | tf_op jit(solution)/shard_map/dot_general | solution.py:357
  70.4 58.7 %shard_map.47.g_ref = f32[512,512]{1,0:T(8,128)} custom-call(f32[512,512]{1,0:T(8,128)} %fusion.14.g_ref), custom_call_target="tpu_custom_call" | custom-call | tf_op jit(solution)/shard_map/pallas_call | solution.py:279
  129.1 58.0 %shard_map.48 = f32[512,512]{1,0:T(8,128)} custom-call(f32[512,512]{1,0:T(8,128)} %shard_map.47.g_ref), custom_call_target="tpu_custom_call" | custom-call | tf_op jit(solution)/shard_map/pallas_call | solution.py:254
  187.2 3.1 %fusion.15 = f32[256,512]{1,0:T(8,128)} fusion(f32[256,512]{1,0:T(8,128)S(1)} %convolution_add_fusion, f32[512,512]{1,0:T(8,128)} %shard_map.48), kind=kOutput, calls=%fused_computation.18 | convolution fusion | flops 805306368 | bytes 2097152 | tf_op jit(solution)/shard_map/dot_general | solution.py:199
Async XLA Ops:
  0.0 41.1 %copy-start = (bf16[2,40,128,128]{3,2,1,0:T(8,128)(2,1)S(1)}, bf16[2,40,128,128]{3,2,1,0:T(8,128)(2,1)}, u32[]{:S(2)}) copy-start(bf16[2,40,128,128]{3,2,1,0:T(8,128)(2,1)} %param.4) | copy-start | bytes 7864324
  32.1 29.5 %collective-permute-start = (bf16[2048,512]{1,0:T(8,128)(2,1)}, bf16[2048,512]{1,0:T(8,128)(2,1)}, u32[]{:S(2)}, u32[]{:S(2)}) collective-permute-start(bf16[2048,512]{1,0:T(8,128)(2,1)} %shard_map.46), channel_id=1, source_target_pairs={{0,8},{8,16},{16,24},{24,32},{32,40},{40,48},{48,56},{56,64},{64,7... | collective-permute-start | bytes 6291464 | tf_op jit(solution)/shard_map/ppermute | solution.py:309
  38.4 27.7 %collective-permute-start.1 = (bf16[2048,512]{1,0:T(8,128)(2,1)}, bf16[2048,512]{1,0:T(8,128)(2,1)}, u32[]{:S(2)}, u32[]{:S(2)}) collective-permute-start(bf16[2048,512]{1,0:T(8,128)(2,1)} %shard_map.46), channel_id=1, source_target_pairs={{8,0},{16,8},{24,16},{32,24},{40,32},{48,40},{56,48},{64,56},{72,6... | collective-permute-start | bytes 6291464 | tf_op jit(solution)/shard_map/ppermute | solution.py:310
  43.8 1.6 copy-start.1

commit v6 on v5

--- a/solution.py
+++ b/solution.py
@@ -209,29 +209,24 @@
     lane = lax.broadcasted_iota(jnp.int32, (1, t), 1)
     eye = (lax.broadcasted_iota(jnp.int32, (t, t), 0) == lax.broadcasted_iota(jnp.int32, (t, t), 1)).astype(jnp.float32)
 
-    def step(r0, j, carry):
-        lane2 = lax.broadcasted_iota(jnp.int32, (t - r0, t), 1)
-        sub = lax.broadcasted_iota(jnp.int32, (t - r0, 1), 0) + r0
-        row = d_ref[pl.ds(j, 1), :]
-        piv2 = jnp.sum(jnp.where(lane == j, row, 0.0), axis=1, keepdims=True)
-        inv = lax.rsqrt(piv2)
-        dmat = d_ref[r0:, :]
-        colfull = jnp.sum(jnp.where(lane2 == j, dmat, 0.0), axis=1, keepdims=True)
-        col = jnp.where(sub >= j, colfull * inv, 0.0)
-        lrow = jnp.where(lane >= j, row * inv, 0.0)
-        d_ref[r0:, :] = dmat - col * lrow
-        brow = b_ref[pl.ds(j, 1), :] * inv
-        bmat = b_ref[r0:, :]
-        b_ref[r0:, :] = bmat - jnp.where(sub > j, col, 0.0) * brow
-        b_ref[pl.ds(j, 1), :] = brow
-        return carry
-
     for k in range(nb):
         lo = k * t
         d_ref[...] = a_ref[lo:lo + t, lo:lo + t]
         b_ref[...] = eye
         for r0 in range(0, t, 8):
-            lax.fori_loop(r0, r0 + 8, functools.partial(step, r0), 0)
+            sub = lax.broadcasted_iota(jnp.int32, (t - r0, 1), 0) + r0
+            dl = d_ref[r0:, :]
+            bl = b_ref[r0:, :]
+            for i in range(8):
+                j = r0 + i
+                inv = lax.rsqrt(dl[i:i + 1, j:j + 1])
+                col = jnp.where(sub >= j, dl[:, j:j + 1] * inv, 0.0)
+                lrow = jnp.where(lane >= j, dl[i:i + 1, :] * inv, 0.0)
+                dl = dl - col * lrow
+                brow = bl[i:i + 1, :] * inv
+                bl = jnp.where(sub == j, brow, bl - jnp.where(sub > j, col, 0.0) * brow)
+            d_ref[r0:, :] = dl
+            b_ref[r0:, :] = bl
         m_ref[lo:lo + t, lo:lo + t] = b_ref[...]
         if k < nb - 1:
             hi = lo + t

time: 191 us -> 186 us (0.974)
  Pallas kernels: 149 us -> 144 us
    pallas_call x1, Pallas kernels: 58 us -> 53.2 us  [chol_inverse(): pl.pallas_call(functools.partial(_chol_inv_kernel, count), out_shape=jax....]
where the time goes in v6:
time: 186 us; the launch traced here: 185 us
  Pallas kernels  144 us (77%)
  waiting for transfers between devices  17.7 us (10%)
  matrix products  13.1 us (7%)
  starting transfers between devices  8.16 us (4%)
    pallas_call x1, Pallas kernels, gram_allreduce(): pl.pallas_call(functools.partial(_ar_kernel, dims), out_shape=jax.ShapeDt...  58.7 us
    pallas_call x1, Pallas kernels, chol_inverse(): pl.pallas_call(functools.partial(_chol_inv_kernel, count), out_shape=jax....  53.2 us
    pallas_call x1, Pallas kernels, zone_gather(): pl.pallas_call(functools.partial(_zone_gather_kernel, nb), out_shape=jax....  32.1 us
    ppermute x1, waiting for transfers between devices, extended(): before = lax.ppermute(last, axis, up)  15.6 us
    ppermute x1, starting transfers between devices, extended(): before = lax.ppermute(last, axis, up)  6.24 us
    dot_general x3, matrix products, add_columns(): jnp.dot(columns, shard_rows, preferred_element_type=jnp.float32)  5.28 us
  transfers between devices with their start and end apart: 2, of which 2 were waited for; matrix products, arithmetic and copies ran while one was open for 4% of the time, Pallas kernels for 0%

profile of v6, /device:TPU:1, one launch (start us, length us, event | category | flops | bytes accessed | tf_op | source)
XLA Modules:
  0.0 185.4 jit_solution(7475191355349771036)
XLA Ops:
  0.0 0.0 copy-start
  0.0 32.1 %shard_map.46 = bf16[2048,512]{1,0:T(8,128)(2,1)} custom-call(bf16[256,512]{1,0:T(8,128)(2,1)} %p_ref.1), custom_call_target="tpu_custom_call" | custom-call | tf_op jit(solution)/shard_map/pallas_call | solution.py:177
  32.1 6.2 %collective-permute-start = (bf16[2048,512]{1,0:T(8,128)(2,1)}, bf16[2048,512]{1,0:T(8,128)(2,1)}, u32[]{:S(2)}, u32[]{:S(2)}) collective-permute-start(bf16[2048,512]{1,0:T(8,128)(2,1)} %shard_map.46), channel_id=1, source_target_pairs={{0,8},{8,16},{16,24},{24,32},{32,40},{40,48},{48,56},{56,64},{64,7... | collective-permute-start | bytes 6291464 | tf_op jit(solution)/shard_map/ppermute | solution.py:304
  38.4 1.9 %collective-permute-start.1 = (bf16[2048,512]{1,0:T(8,128)(2,1)}, bf16[2048,512]{1,0:T(8,128)(2,1)}, u32[]{:S(2)}, u32[]{:S(2)}) collective-permute-start(bf16[2048,512]{1,0:T(8,128)(2,1)} %shard_map.46), channel_id=1, source_target_pairs={{8,0},{16,8},{24,16},{32,24},{40,32},{48,40},{56,48},{64,56},{72,6... | collective-permute-start | bytes 6291464 | tf_op jit(solution)/shard_map/ppermute | solution.py:305
  40.3 0.8 compare_and_fusion
  41.1 0.0 copy-done
  41.1 2.7 %fusion.2 = bf16[2,48,128,128]{3,1,2,0:T(8,128)(2,1)S(1)} fusion(bf16[2,40,128,128]{3,2,1,0:T(8,128)(2,1)S(1)} %copy-done, s32[2,40]{1,0:T(2,128)S(1)} %get-tuple-element.6, pred[2,40]{1,0:T(4,128)(4,1)S(1)} %get-tuple-element.5), kind=kOutput, calls=%fused_computation.3 | convolution fusion | flops 127409664 | bytes 5767568 | tf_op jit(solution)/shard_map/lsp,lsac->lapc/dot_general | solution.py:329
  43.8 0.0 copy-start.1
  43.8 0.8 copy.13
  44.6 0.8 copy-done.1
  45.3 0.7 fusion.7
  46.0 15.6 %collective-permute-done = bf16[2048,512]{1,0:T(8,128)(2,1)} collective-permute-done((bf16[2048,512]{1,0:T(8,128)(2,1)}, bf16[2048,512]{1,0:T(8,128)(2,1)}, u32[]{:S(2)}, u32[]{:S(2)}) %collective-permute-start) | collective-permute-done | bytes 2097184 | tf_op jit(solution)/shard_map/ppermute | solution.py:304
  61.6 2.3 %convolution_add_fusion.1 = f32[256,512]{1,0:T(8,128)S(1)} fusion(f32[256,512]{1,0:T(8,128)S(1)} %fusion.7, bf16[2048,512]{1,0:T(8,128)(2,1)} %collective-permute-done, bf16[256,6144]{1,0:T(8,128)(2,1)S(1)} %bitcast.20), kind=kOutput, calls=%fused_computation.5 | convolution fusion | flops 537001984 | bytes 4194304 | tf_op jit(solution)/shard_map/dot_general | solution.py:339
  63.9 2.1 %collective-permute-done.1 = bf16[2048,512]{1,0:T(8,128)(2,1)} collective-permute-done((bf16[2048,512]{1,0:T(8,128)(2,1)}, bf16[2048,512]{1,0:T(8,128)(2,1)}, u32[]{:S(2)}, u32[]{:S(2)}) %collective-permute-start.1) | collective-permute-done | bytes 2097184 | tf_op jit(solution)/shard_map/ppermute | solution.py:305
  66.0 2.3 %convolution_add_fusion = f32[256,512]{1,0:T(8,128)S(1)} fusion(f32[256,512]{1,0:T(8,128)S(1)} %convolution_add_fusion.1, bf16[2048,512]{1,0:T(8,128)(2,1)} %collective-permute-done.1, bf16[256,6144]{1,0:T(8,128)(2,1)S(1)} %bitcast.21), kind=kOutput, calls=%fused_computation.4 | convolution fusion | flops 537001984 | bytes 4194304 | tf_op jit(solution)/shard_map/dot_general | solution.py:339
  68.3 2.1 %fusion.14.g_ref = f32[512,512]{1,0:T(8,128)} fusion(f32[256,512]{1,0:T(8,128)S(1)} %convolution_add_fusion), kind=kOutput, calls=%fused_computation.17 | convolution fusion | flops 805306368 | bytes 1572864 | tf_op jit(solution)/shard_map/dot_general | solution.py:352
  70.4 58.7 %shard_map.47.g_ref = f32[512,512]{1,0:T(8,128)} custom-call(f32[512,512]{1,0:T(8,128)} %fusion.14.g_ref), custom_call_target="tpu_custom_call" | custom-call | tf_op jit(solution)/shard_map/pallas_call | solution.py:274
  129.1 53.2 %shard_map.48 = f32[512,512]{1,0:T(8,128)} custom-call(f32[512,512]{1,0:T(8,128)} %shard_map.47.g_ref), custom_call_target="tpu_custom_call" | custom-call | tf_op jit(solution)/shard_map/pallas_call | solution.py:249
  182.3 3.1 %fusion.15 = f32[256,512]{1,0:T(8,128)} fusion(f32[256,512]{1,0:T(8,128)S(1)} %convolution_add_fusion, f32[512,512]{1,0:T(8,128)} %shard_map.48), kind=kOutput, calls=%fused_computation.18 | convolution fusion | flops 805306368 | bytes 2097152 | tf_op jit(solution)/shard_map/dot_general | solution.py:199
Async XLA Ops:
  0.0 41.1 %copy-start = (bf16[2,40,128,128]{3,2,1,0:T(8,128)(2,1)S(1)}, bf16[2,40,128,128]{3,2,1,0:T(8,128)(2,1)}, u32[]{:S(2)}) copy-start(bf16[2,40,128,128]{3,2,1,0:T(8,128)(2,1)} %param.4) | copy-start | bytes 7864324
  32.1 29.5 %collective-permute-start = (bf16[2048,512]{1,0:T(8,128)(2,1)}, bf16[2048,512]{1,0:T(8,128)(2,1)}, u32[]{:S(2)}, u32[]{:S(2)}) collective-permute-start(bf16[2048,512]{1,0:T(8,128)(2,1)} %shard_map.46), channel_id=1, source_target_pairs={{0,8},{8,16},{16,24},{24,32},{32,40},{40,48},{48,56},{56,64},{64,7... | collective-permute-start | bytes 6291464 | tf_op jit(solution)/shard_map/ppermute | solution.py:304
  38.4 27.7 %collective-permute-start.1 = (bf16[2048,512]{1,0:T(8,128)(2,1)}, bf16[2048,512]{1,0:T(8,128)(2,1)}, u32[]{:S(2)}, u32[]{:S(2)}) collective-permute-start(bf16[2048,512]{1,0:T(8,128)(2,1)} %shard_map.46), channel_id=1, source_target_pairs={{8,0},{16,8},{24,16},{32,24},{40,32},{48,40},{56,48},{64,56},{72,6... | collective-permute-start | bytes 6291464 | tf_op jit(solution)/shard_map/ppermute | solution.py:305
  43.8 1.6 copy-start.1

commit v7 on v6

--- a/solution.py
+++ b/solution.py
@@ -141,7 +141,8 @@
     wait_recv(full.at[mine], full.at[rows((1 - c) * S1, S1)], o_agc, core_peer)
     d.wait_send()
 
-    out_ref[...] = full[...]
+    if out_ref is not None:
+        out_ref[...] = full[...]
 
 
 def _zone_gather_kernel(nb, p_ref, out_ref, ssem, rsem, lsem):
@@ -243,24 +244,7 @@
             m_ref[i * t:(i + 1) * t, j * t:(j + 1) * t] = -_mm(m_ref[i * t:(i + 1) * t, i * t:(i + 1) * t], acc)
 
 
-def chol_inverse(g, count, t=128):
-    n = g.shape[0]
-    vmem = pltpu.VMEM
-    return pl.pallas_call(
-        functools.partial(_chol_inv_kernel, count),
-        out_shape=jax.ShapeDtypeStruct((n, n), jnp.float32),
-        in_specs=[pl.BlockSpec(memory_space=vmem)],
-        out_specs=pl.BlockSpec(memory_space=vmem),
-        scratch_shapes=[
-            vmem((n, n), jnp.float32),
-            vmem((t, t), jnp.float32),
-            vmem((t, t), jnp.float32),
-            vmem((n, n), jnp.float32),
-        ],
-    )(g)
-
-
-def gram_allreduce(g, dims):
+def gram_factor_inverse(g, dims, count, t=128):
     XL, Z, C, XH, Y = dims
     X = XL * XH
     ZH = Z // 2
@@ -271,8 +255,13 @@
     S4 = S3 // 2
     nsem = 4 + 2 * Y + 2 * X + ZH
     vmem = pltpu.VMEM
+
+    def kernel(g_ref, m_ref, rc, ry, rx, rzl, rzh, a1, a2, a3, a4, full, ssem, rsem, ca, cd, cb, cl):
+        _ar_kernel(dims, g_ref, None, rc, ry, rx, rzl, rzh, a1, a2, a3, a4, full, ssem, rsem)
+        _chol_inv_kernel(count, full, m_ref, ca, cd, cb, cl)
+
     return pl.pallas_call(
-        functools.partial(_ar_kernel, dims),
+        kernel,
         out_shape=jax.ShapeDtypeStruct((N, M), jnp.float32),
         in_specs=[pl.BlockSpec(memory_space=vmem)],
         out_specs=pl.BlockSpec(memory_space=vmem),
@@ -289,6 +278,10 @@
             vmem((N, M), jnp.float32),
             pltpu.SemaphoreType.DMA((nsem,)),
             pltpu.SemaphoreType.DMA((nsem,)),
+            vmem((N, N), jnp.float32),
+            vmem((t, t), jnp.float32),
+            vmem((t, t), jnp.float32),
+            vmem((N, N), jnp.float32),
         ],
         compiler_params=pltpu.CompilerParams(collective_id=0, has_side_effects=True),
     )(g)
@@ -356,9 +349,8 @@
         precision=lax.Precision.HIGHEST,
         preferred_element_type=jnp.float32,
     )
-    gram_total = gram_allreduce(gram_local, _dims())
     point_count = tile_rows * lax.axis_size("rows") * lax.axis_size("blk")
-    factor_inverse = chol_inverse(gram_total, float(point_count))
+    factor_inverse = gram_factor_inverse(gram_local, _dims(), float(point_count))
     return _mm_t(images, factor_inverse)
 
 

time: 186 us -> 183 us (0.984)
  Pallas kernels: 144 us -> 142 us
    pallas_call x2 -> x1, Pallas kernels: 112 us -> 110 us  [gram_factor_inverse(): pl.pallas_call(kernel, out_shape=jax.ShapeDtypeStruct((N, M), jnp.float32...]
where the time goes in v7:
time: 183 us
  Pallas kernels  142 us (78%)
  waiting for transfers between devices  17.7 us (10%)
  matrix products  13 us (7%)
  starting transfers between devices  8.16 us (4%)
    pallas_call x1, Pallas kernels, gram_factor_inverse(): pl.pallas_call(kernel, out_shape=jax.ShapeDtypeStruct((N, M), jnp.float32...  110 us
    pallas_call x1, Pallas kernels, zone_gather(): pl.pallas_call(functools.partial(_zone_gather_kernel, nb), out_shape=jax....  32.1 us
    ppermute x1, waiting for transfers between devices, extended(): before = lax.ppermute(last, axis, up)  15.6 us
    ppermute x1, starting transfers between devices, extended(): before = lax.ppermute(last, axis, up)  6.24 us
    dot_general x3, matrix products, add_columns(): jnp.dot(columns, shard_rows, preferred_element_type=jnp.float32)  5.28 us
  transfers between devices with their start and end apart: 2, of which 2 were waited for; matrix products, arithmetic and copies ran while one was open for 4% of the time, Pallas kernels for 0%

profile of v7, /device:TPU:1, one launch (start us, length us, event | category | flops | bytes accessed | tf_op | source)
XLA Modules:
  0.0 183.0 jit_solution(16690037175122345047)
XLA Ops:
  0.0 0.0 copy-start
  0.0 32.1 %shard_map.46 = bf16[2048,512]{1,0:T(8,128)(2,1)} custom-call(bf16[256,512]{1,0:T(8,128)(2,1)} %p_ref.1), custom_call_target="tpu_custom_call" | custom-call | tf_op jit(solution)/shard_map/pallas_call | solution.py:178
  32.1 6.2 %collective-permute-start = (bf16[2048,512]{1,0:T(8,128)(2,1)}, bf16[2048,512]{1,0:T(8,128)(2,1)}, u32[]{:S(2)}, u32[]{:S(2)}) collective-permute-start(bf16[2048,512]{1,0:T(8,128)(2,1)} %shard_map.46), channel_id=1, source_target_pairs={{0,8},{8,16},{16,24},{24,32},{32,40},{40,48},{48,56},{56,64},{64,7... | collective-permute-start | bytes 6291464 | tf_op jit(solution)/shard_map/ppermute | solution.py:297
  38.4 1.9 %collective-permute-start.1 = (bf16[2048,512]{1,0:T(8,128)(2,1)}, bf16[2048,512]{1,0:T(8,128)(2,1)}, u32[]{:S(2)}, u32[]{:S(2)}) collective-permute-start(bf16[2048,512]{1,0:T(8,128)(2,1)} %shard_map.46), channel_id=1, source_target_pairs={{8,0},{16,8},{24,16},{32,24},{40,32},{48,40},{56,48},{64,56},{72,6... | collective-permute-start | bytes 6291464 | tf_op jit(solution)/shard_map/ppermute | solution.py:298
  40.3 0.8 compare_and_fusion
  41.1 0.0 copy-done
  41.1 2.7 %fusion.2 = bf16[2,48,128,128]{3,1,2,0:T(8,128)(2,1)S(1)} fusion(bf16[2,40,128,128]{3,2,1,0:T(8,128)(2,1)S(1)} %copy-done, s32[2,40]{1,0:T(2,128)S(1)} %get-tuple-element.6, pred[2,40]{1,0:T(4,128)(4,1)S(1)} %get-tuple-element.5), kind=kOutput, calls=%fused_computation.3 | convolution fusion | flops 127409664 | bytes 5767568 | tf_op jit(solution)/shard_map/lsp,lsac->lapc/dot_general | solution.py:322
  43.8 0.0 copy-start.1
  43.8 0.8 copy.13
  44.6 0.8 copy-done.1
  45.3 0.7 fusion.7
  46.0 15.6 %collective-permute-done = bf16[2048,512]{1,0:T(8,128)(2,1)} collective-permute-done((bf16[2048,512]{1,0:T(8,128)(2,1)}, bf16[2048,512]{1,0:T(8,128)(2,1)}, u32[]{:S(2)}, u32[]{:S(2)}) %collective-permute-start) | collective-permute-done | bytes 2097184 | tf_op jit(solution)/shard_map/ppermute | solution.py:297
  61.6 2.3 %convolution_add_fusion.1 = f32[256,512]{1,0:T(8,128)S(1)} fusion(f32[256,512]{1,0:T(8,128)S(1)} %fusion.7, bf16[2048,512]{1,0:T(8,128)(2,1)} %collective-permute-done, bf16[256,6144]{1,0:T(8,128)(2,1)S(1)} %bitcast.20), kind=kOutput, calls=%fused_computation.5 | convolution fusion | flops 537001984 | bytes 4194304 | tf_op jit(solution)/shard_map/dot_general | solution.py:332
  63.9 2.1 %collective-permute-done.1 = bf16[2048,512]{1,0:T(8,128)(2,1)} collective-permute-done((bf16[2048,512]{1,0:T(8,128)(2,1)}, bf16[2048,512]{1,0:T(8,128)(2,1)}, u32[]{:S(2)}, u32[]{:S(2)}) %collective-permute-start.1) | collective-permute-done | bytes 2097184 | tf_op jit(solution)/shard_map/ppermute | solution.py:298
  66.0 2.3 %convolution_add_fusion = f32[256,512]{1,0:T(8,128)S(1)} fusion(f32[256,512]{1,0:T(8,128)S(1)} %convolution_add_fusion.1, bf16[2048,512]{1,0:T(8,128)(2,1)} %collective-permute-done.1, bf16[256,6144]{1,0:T(8,128)(2,1)S(1)} %bitcast.21), kind=kOutput, calls=%fused_computation.4 | convolution fusion | flops 537001984 | bytes 4194304 | tf_op jit(solution)/shard_map/dot_general | solution.py:332
  68.3 2.0 %fusion.14.g_ref = f32[512,512]{1,0:T(8,128)} fusion(f32[256,512]{1,0:T(8,128)S(1)} %convolution_add_fusion), kind=kOutput, calls=%fused_computation.17 | convolution fusion | flops 805306368 | bytes 1572864 | tf_op jit(solution)/shard_map/dot_general | solution.py:345
  70.3 109.6 %shard_map.47 = f32[512,512]{1,0:T(8,128)} custom-call(f32[512,512]{1,0:T(8,128)} %fusion.14.g_ref), custom_call_target="tpu_custom_call" | custom-call | tf_op jit(solution)/shard_map/pallas_call | solution.py:263
  179.9 3.1 %fusion.15 = f32[256,512]{1,0:T(8,128)} fusion(f32[256,512]{1,0:T(8,128)S(1)} %convolution_add_fusion, f32[512,512]{1,0:T(8,128)} %shard_map.47), kind=kOutput, calls=%fused_computation.18 | convolution fusion | flops 805306368 | bytes 2097152 | tf_op jit(solution)/shard_map/dot_general | solution.py:200
Async XLA Ops:
  0.0 41.1 %copy-start = (bf16[2,40,128,128]{3,2,1,0:T(8,128)(2,1)S(1)}, bf16[2,40,128,128]{3,2,1,0:T(8,128)(2,1)}, u32[]{:S(2)}) copy-start(bf16[2,40,128,128]{3,2,1,0:T(8,128)(2,1)} %param.4) | copy-start | bytes 7864324
  32.1 29.5 %collective-permute-start = (bf16[2048,512]{1,0:T(8,128)(2,1)}, bf16[2048,512]{1,0:T(8,128)(2,1)}, u32[]{:S(2)}, u32[]{:S(2)}) collective-permute-start(bf16[2048,512]{1,0:T(8,128)(2,1)} %shard_map.46), channel_id=1, source_target_pairs={{0,8},{8,16},{16,24},{24,32},{32,40},{40,48},{48,56},{56,64},{64,7... | collective-permute-start | bytes 6291464 | tf_op jit(solution)/shard_map/ppermute | solution.py:297
  38.4 27.7 %collective-permute-start.1 = (bf16[2048,512]{1,0:T(8,128)(2,1)}, bf16[2048,512]{1,0:T(8,128)(2,1)}, u32[]{:S(2)}, u32[]{:S(2)}) collective-permute-start(bf16[2048,512]{1,0:T(8,128)(2,1)} %shard_map.46), channel_id=1, source_target_pairs={{8,0},{16,8},{24,16},{32,24},{40,32},{48,40},{56,48},{64,56},{72,6... | collective-permute-start | bytes 6291464 | tf_op jit(solution)/shard_map/ppermute | solution.py:298
  43.8 1.6 copy-start.1

commit v8 on v7

--- a/solution.py
+++ b/solution.py
@@ -214,11 +214,11 @@
         lo = k * t
         d_ref[...] = a_ref[lo:lo + t, lo:lo + t]
         b_ref[...] = eye
-        for r0 in range(0, t, 8):
+        for r0 in range(0, t, 16):
             sub = lax.broadcasted_iota(jnp.int32, (t - r0, 1), 0) + r0
             dl = d_ref[r0:, :]
             bl = b_ref[r0:, :]
-            for i in range(8):
+            for i in range(16):
                 j = r0 + i
                 inv = lax.rsqrt(dl[i:i + 1, j:j + 1])
                 col = jnp.where(sub >= j, dl[:, j:j + 1] * inv, 0.0)

time: 183 us -> 183 us (level)
  no operation moved by 1% of the time
where the time goes in v8:
time: 183 us
  Pallas kernels  142 us (78%)
  waiting for transfers between devices  17.7 us (10%)
  matrix products  13 us (7%)
  starting transfers between devices  8.16 us (4%)
    pallas_call x1, Pallas kernels, gram_factor_inverse(): pl.pallas_call(kernel, out_shape=jax.ShapeDtypeStruct((N, M), jnp.float32...  110 us
    pallas_call x1, Pallas kernels, zone_gather(): pl.pallas_call(functools.partial(_zone_gather_kernel, nb), out_shape=jax....  32.1 us
    ppermute x1, waiting for transfers between devices, extended(): before = lax.ppermute(last, axis, up)  15.6 us
    ppermute x1, starting transfers between devices, extended(): before = lax.ppermute(last, axis, up)  6.24 us
    dot_general x3, matrix products, add_columns(): jnp.dot(columns, shard_rows, preferred_element_type=jnp.float32)  5.28 us
  transfers between devices with their start and end apart: 2, of which 2 were waited for; matrix products, arithmetic and copies ran while one was open for 4% of the time, Pallas kernels for 0%

profile of v8, /device:TPU:1, one launch (start us, length us, event | category | flops | bytes accessed | tf_op | source)
XLA Modules:
  0.0 183.1 jit_solution(5746217694978975952)
XLA Ops:
  0.0 0.0 copy-start
  0.0 32.1 %shard_map.46 = bf16[2048,512]{1,0:T(8,128)(2,1)} custom-call(bf16[256,512]{1,0:T(8,128)(2,1)} %p_ref.1), custom_call_target="tpu_custom_call" | custom-call | tf_op jit(solution)/shard_map/pallas_call | solution.py:178
  32.1 6.2 %collective-permute-start = (bf16[2048,512]{1,0:T(8,128)(2,1)}, bf16[2048,512]{1,0:T(8,128)(2,1)}, u32[]{:S(2)}, u32[]{:S(2)}) collective-permute-start(bf16[2048,512]{1,0:T(8,128)(2,1)} %shard_map.46), channel_id=1, source_target_pairs={{0,8},{8,16},{16,24},{24,32},{32,40},{40,48},{48,56},{56,64},{64,7... | collective-permute-start | bytes 6291464 | tf_op jit(solution)/shard_map/ppermute | solution.py:297
  38.4 1.9 %collective-permute-start.1 = (bf16[2048,512]{1,0:T(8,128)(2,1)}, bf16[2048,512]{1,0:T(8,128)(2,1)}, u32[]{:S(2)}, u32[]{:S(2)}) collective-permute-start(bf16[2048,512]{1,0:T(8,128)(2,1)} %shard_map.46), channel_id=1, source_target_pairs={{8,0},{16,8},{24,16},{32,24},{40,32},{48,40},{56,48},{64,56},{72,6... | collective-permute-start | bytes 6291464 | tf_op jit(solution)/shard_map/ppermute | solution.py:298
  40.3 0.8 compare_and_fusion
  41.1 0.0 copy-done
  41.1 2.7 %fusion.2 = bf16[2,48,128,128]{3,1,2,0:T(8,128)(2,1)S(1)} fusion(bf16[2,40,128,128]{3,2,1,0:T(8,128)(2,1)S(1)} %copy-done, s32[2,40]{1,0:T(2,128)S(1)} %get-tuple-element.6, pred[2,40]{1,0:T(4,128)(4,1)S(1)} %get-tuple-element.5), kind=kOutput, calls=%fused_computation.3 | convolution fusion | flops 127409664 | bytes 5767568 | tf_op jit(solution)/shard_map/lsp,lsac->lapc/dot_general | solution.py:322
  43.8 0.0 copy-start.1
  43.8 0.8 copy.13
  44.6 0.8 copy-done.1
  45.3 0.7 fusion.7
  46.0 15.6 %collective-permute-done = bf16[2048,512]{1,0:T(8,128)(2,1)} collective-permute-done((bf16[2048,512]{1,0:T(8,128)(2,1)}, bf16[2048,512]{1,0:T(8,128)(2,1)}, u32[]{:S(2)}, u32[]{:S(2)}) %collective-permute-start) | collective-permute-done | bytes 2097184 | tf_op jit(solution)/shard_map/ppermute | solution.py:297
  61.6 2.3 %convolution_add_fusion.1 = f32[256,512]{1,0:T(8,128)S(1)} fusion(f32[256,512]{1,0:T(8,128)S(1)} %fusion.7, bf16[2048,512]{1,0:T(8,128)(2,1)} %collective-permute-done, bf16[256,6144]{1,0:T(8,128)(2,1)S(1)} %bitcast.20), kind=kOutput, calls=%fused_computation.5 | convolution fusion | flops 537001984 | bytes 4194304 | tf_op jit(solution)/shard_map/dot_general | solution.py:332
  63.9 2.1 %collective-permute-done.1 = bf16[2048,512]{1,0:T(8,128)(2,1)} collective-permute-done((bf16[2048,512]{1,0:T(8,128)(2,1)}, bf16[2048,512]{1,0:T(8,128)(2,1)}, u32[]{:S(2)}, u32[]{:S(2)}) %collective-permute-start.1) | collective-permute-done | bytes 2097184 | tf_op jit(solution)/shard_map/ppermute | solution.py:298
  66.0 2.3 %convolution_add_fusion = f32[256,512]{1,0:T(8,128)S(1)} fusion(f32[256,512]{1,0:T(8,128)S(1)} %convolution_add_fusion.1, bf16[2048,512]{1,0:T(8,128)(2,1)} %collective-permute-done.1, bf16[256,6144]{1,0:T(8,128)(2,1)S(1)} %bitcast.21), kind=kOutput, calls=%fused_computation.4 | convolution fusion | flops 537001984 | bytes 4194304 | tf_op jit(solution)/shard_map/dot_general | solution.py:332
  68.3 2.0 %fusion.14.g_ref = f32[512,512]{1,0:T(8,128)} fusion(f32[256,512]{1,0:T(8,128)S(1)} %convolution_add_fusion), kind=kOutput, calls=%fused_computation.17 | convolution fusion | flops 805306368 | bytes 1572864 | tf_op jit(solution)/shard_map/dot_general | solution.py:345
  70.3 109.7 %shard_map.47 = f32[512,512]{1,0:T(8,128)} custom-call(f32[512,512]{1,0:T(8,128)} %fusion.14.g_ref), custom_call_target="tpu_custom_call" | custom-call | tf_op jit(solution)/shard_map/pallas_call | solution.py:263
  180.0 3.1 %fusion.15 = f32[256,512]{1,0:T(8,128)} fusion(f32[256,512]{1,0:T(8,128)S(1)} %convolution_add_fusion, f32[512,512]{1,0:T(8,128)} %shard_map.47), kind=kOutput, calls=%fused_computation.18 | convolution fusion | flops 805306368 | bytes 2097152 | tf_op jit(solution)/shard_map/dot_general | solution.py:200
Async XLA Ops:
  0.0 41.1 %copy-start = (bf16[2,40,128,128]{3,2,1,0:T(8,128)(2,1)S(1)}, bf16[2,40,128,128]{3,2,1,0:T(8,128)(2,1)}, u32[]{:S(2)}) copy-start(bf16[2,40,128,128]{3,2,1,0:T(8,128)(2,1)} %param.4) | copy-start | bytes 7864324
  32.1 29.5 %collective-permute-start = (bf16[2048,512]{1,0:T(8,128)(2,1)}, bf16[2048,512]{1,0:T(8,128)(2,1)}, u32[]{:S(2)}, u32[]{:S(2)}) collective-permute-start(bf16[2048,512]{1,0:T(8,128)(2,1)} %shard_map.46), channel_id=1, source_target_pairs={{0,8},{8,16},{16,24},{24,32},{32,40},{40,48},{48,56},{56,64},{64,7... | collective-permute-start | bytes 6291464 | tf_op jit(solution)/shard_map/ppermute | solution.py:297
  38.4 27.7 %collective-permute-start.1 = (bf16[2048,512]{1,0:T(8,128)(2,1)}, bf16[2048,512]{1,0:T(8,128)(2,1)}, u32[]{:S(2)}, u32[]{:S(2)}) collective-permute-start(bf16[2048,512]{1,0:T(8,128)(2,1)} %shard_map.46), channel_id=1, source_target_pairs={{8,0},{16,8},{24,16},{32,24},{40,32},{48,40},{56,48},{64,56},{72,6... | collective-permute-start | bytes 6291464 | tf_op jit(solution)/shard_map/ppermute | solution.py:298
  43.8 1.6 copy-start.1

commit v9 on v7

--- a/solution.py
+++ b/solution.py
@@ -9,7 +9,7 @@
 MESH_ID = pl.DeviceIdType.MESH
 
 
-def _ar_kernel(dims, g_ref, out_ref, rc, ry, rx, rzl, rzh, a1, a2, a3, a4, full, ssem, rsem):
+def _ar_kernel(dims, g_ref, out_ref, rc, ry, rx, rzl, rzh, a1, a2, a3, a4, full, ssem, rsem, prologue=None):
     XL, Z, C, XH, Y = dims
     X = XL * XH
     ZH = Z // 2
@@ -45,6 +45,8 @@
     barrier = pltpu.get_barrier_semaphore()
     for p in peers:
         pl.semaphore_signal(barrier, inc=1, device_id=p, device_id_type=MESH_ID)
+    if prologue is not None:
+        prologue()
     pl.semaphore_wait(barrier, len(peers))
 
     o_core, o_y, o_x, o_zl, o_zh = 0, 1, 1 + Y, 1 + Y + X, 2 + Y + X
@@ -244,11 +246,11 @@
             m_ref[i * t:(i + 1) * t, j * t:(j + 1) * t] = -_mm(m_ref[i * t:(i + 1) * t, i * t:(i + 1) * t], acc)
 
 
-def gram_factor_inverse(g, dims, count, t=128):
+def orthonormal_basis(images, dims, count, t=128):
     XL, Z, C, XH, Y = dims
     X = XL * XH
     ZH = Z // 2
-    N, M = g.shape
+    N = M = images.shape[1]
     S1 = N // C
     S2 = S1 // Y
     S3 = S2 // X
@@ -256,13 +258,18 @@
     nsem = 4 + 2 * Y + 2 * X + ZH
     vmem = pltpu.VMEM
 
-    def kernel(g_ref, m_ref, rc, ry, rx, rzl, rzh, a1, a2, a3, a4, full, ssem, rsem, ca, cd, cb, cl):
-        _ar_kernel(dims, g_ref, None, rc, ry, rx, rzl, rzh, a1, a2, a3, a4, full, ssem, rsem)
-        _chol_inv_kernel(count, full, m_ref, ca, cd, cb, cl)
+    def kernel(x_ref, out_ref, rc, ry, rx, rzl, rzh, a1, a2, a3, a4, full, ssem, rsem, ca, cd, cb, cl, gsc, msc):
+        def local_gram():
+            x = x_ref[...]
+            gsc[...] = jnp.dot(x.T, x, precision=HI, preferred_element_type=jnp.float32)
+
+        _ar_kernel(dims, gsc, None, rc, ry, rx, rzl, rzh, a1, a2, a3, a4, full, ssem, rsem, local_gram)
+        _chol_inv_kernel(count, full, msc, ca, cd, cb, cl)
+        out_ref[...] = _mm_t(x_ref[...], msc[...])
 
     return pl.pallas_call(
         kernel,
-        out_shape=jax.ShapeDtypeStruct((N, M), jnp.float32),
+        out_shape=jax.ShapeDtypeStruct(images.shape, jnp.float32),
         in_specs=[pl.BlockSpec(memory_space=vmem)],
         out_specs=pl.BlockSpec(memory_space=vmem),
         scratch_shapes=[
@@ -282,9 +289,11 @@
             vmem((t, t), jnp.float32),
             vmem((t, t), jnp.float32),
             vmem((N, N), jnp.float32),
+            vmem((N, N), jnp.float32),
+            vmem((N, N), jnp.float32),
         ],
         compiler_params=pltpu.CompilerParams(collective_id=0, has_side_effects=True),
-    )(g)
+    )(images)
 
 
 def extended(x, sides, width):
@@ -342,16 +351,8 @@
         lax.slice_in_dim(near_zones, 2 * zone_length, 3 * zone_length, axis=0),
         2 * zone_length,
     )
-    gram_local = lax.dot_general(
-        images,
-        images,
-        (((0,), (0,)), ((), ())),
-        precision=lax.Precision.HIGHEST,
-        preferred_element_type=jnp.float32,
-    )
     point_count = tile_rows * lax.axis_size("rows") * lax.axis_size("blk")
-    factor_inverse = gram_factor_inverse(gram_local, _dims(), float(point_count))
-    return _mm_t(images, factor_inverse)
+    return orthonormal_basis(images, _dims(), float(point_count))
 
 
 def solution(mesh):

time: 183 us -> 182 us (level)
  matrix products: 13 us -> 8.75 us
  local copies, waits for them, and re-layouts: 1.58 us -> 3.45 us
    dot_general x2 -> x0, matrix products: 5.09 us -> none  [the longest x1 3.08 us: _mm_t(): lax.dot_general(a, b, (((1,), (1,)), ((), ())), precision=HI, preferred_e...]
    unnamed x5 -> x6, local copies, waits for them, and re-layouts: 1.58 us -> 3.45 us
where the time goes in v9:
time: 182 us; the launch traced here: 181 us
  Pallas kernels  143 us (79%)
  waiting for transfers between devices  17.7 us (10%)
  matrix products  8.75 us (5%)
  starting transfers between devices  8.16 us (4%)
  local copies, waits for them, and re-layouts  3.45 us (2%)
    pallas_call x1, Pallas kernels, orthonormal_basis(): pl.pallas_call(kernel, out_shape=jax.ShapeDtypeStruct(images.shape, jnp.f...  110 us
    pallas_call x1, Pallas kernels, zone_gather(): pl.pallas_call(functools.partial(_zone_gather_kernel, nb), out_shape=jax....  32.1 us
    ppermute x1, waiting for transfers between devices, extended(): before = lax.ppermute(last, axis, up)  15.6 us
    ppermute x1, starting transfers between devices, extended(): before = lax.ppermute(last, axis, up)  6.24 us
    dot_general x3, matrix products, add_columns(): jnp.dot(columns, shard_rows, preferred_element_type=jnp.float32)  6.08 us
  transfers between devices with their start and end apart: 2, of which 2 were waited for; matrix products, arithmetic and copies ran while one was open for 4% of the time, Pallas kernels for 0%

profile of v9, /device:TPU:1, one launch (start us, length us, event | category | flops | bytes accessed | tf_op | source)
XLA Modules:
  0.0 181.4 jit_solution(14372252910018649781)
XLA Ops:
  0.0 0.0 copy-start
  0.0 32.1 %shard_map.46 = bf16[2048,512]{1,0:T(8,128)(2,1)} custom-call(bf16[256,512]{1,0:T(8,128)(2,1)} %p_ref.1), custom_call_target="tpu_custom_call" | custom-call | tf_op jit(solution)/shard_map/pallas_call | solution.py:180
  32.1 6.2 %collective-permute-start = (bf16[2048,512]{1,0:T(8,128)(2,1)}, bf16[2048,512]{1,0:T(8,128)(2,1)}, u32[]{:S(2)}, u32[]{:S(2)}) collective-permute-start(bf16[2048,512]{1,0:T(8,128)(2,1)} %shard_map.46), channel_id=1, source_target_pairs={{0,8},{8,16},{16,24},{24,32},{32,40},{40,48},{48,56},{56,64},{64,7... | collective-permute-start | bytes 6291464 | tf_op jit(solution)/shard_map/ppermute | solution.py:306
  38.4 1.9 %collective-permute-start.1 = (bf16[2048,512]{1,0:T(8,128)(2,1)}, bf16[2048,512]{1,0:T(8,128)(2,1)}, u32[]{:S(2)}, u32[]{:S(2)}) collective-permute-start(bf16[2048,512]{1,0:T(8,128)(2,1)} %shard_map.46), channel_id=1, source_target_pairs={{8,0},{16,8},{24,16},{32,24},{40,32},{48,40},{56,48},{64,56},{72,6... | collective-permute-start | bytes 6291464 | tf_op jit(solution)/shard_map/ppermute | solution.py:307
  40.3 0.8 compare_and_fusion
  41.1 0.0 copy-done
  41.1 2.7 %fusion.2 = bf16[2,48,128,128]{3,1,2,0:T(8,128)(2,1)S(1)} fusion(bf16[2,40,128,128]{3,2,1,0:T(8,128)(2,1)S(1)} %copy-done, s32[2,40]{1,0:T(2,128)S(1)} %get-tuple-element.6, pred[2,40]{1,0:T(4,128)(4,1)S(1)} %get-tuple-element.5), kind=kOutput, calls=%fused_computation.3 | convolution fusion | flops 127409664 | bytes 5767568 | tf_op jit(solution)/shard_map/lsp,lsac->lapc/dot_general | solution.py:331
  43.8 0.0 copy-start.1
  43.8 0.8 copy.13
  44.6 0.8 copy-done.1
  45.3 0.7 fusion.7
  46.0 15.6 %collective-permute-done = bf16[2048,512]{1,0:T(8,128)(2,1)} collective-permute-done((bf16[2048,512]{1,0:T(8,128)(2,1)}, bf16[2048,512]{1,0:T(8,128)(2,1)}, u32[]{:S(2)}, u32[]{:S(2)}) %collective-permute-start) | collective-permute-done | bytes 2097184 | tf_op jit(solution)/shard_map/ppermute | solution.py:306
  61.6 2.3 %convolution_add_fusion.1 = f32[256,512]{1,0:T(8,128)S(1)} fusion(f32[256,512]{1,0:T(8,128)S(1)} %fusion.7, bf16[2048,512]{1,0:T(8,128)(2,1)} %collective-permute-done, bf16[256,6144]{1,0:T(8,128)(2,1)S(1)} %bitcast.16), kind=kOutput, calls=%fused_computation.5 | convolution fusion | flops 537001984 | bytes 4194304 | tf_op jit(solution)/shard_map/dot_general | solution.py:341
  63.9 2.1 %collective-permute-done.1 = bf16[2048,512]{1,0:T(8,128)(2,1)} collective-permute-done((bf16[2048,512]{1,0:T(8,128)(2,1)}, bf16[2048,512]{1,0:T(8,128)(2,1)}, u32[]{:S(2)}, u32[]{:S(2)}) %collective-permute-start.1) | collective-permute-done | bytes 2097184 | tf_op jit(solution)/shard_map/ppermute | solution.py:307
  66.0 3.1 %convolution_add_fusion.x_ref = f32[256,512]{1,0:T(8,128)} fusion(f32[256,512]{1,0:T(8,128)S(1)} %convolution_add_fusion.1, bf16[2048,512]{1,0:T(8,128)(2,1)} %collective-permute-done.1, bf16[256,6144]{1,0:T(8,128)(2,1)S(1)} %bitcast.17), kind=kOutput, calls=%fused_computation.4 | convolution fusion | flops 537001984 | bytes 4194304 | tf_op jit(solution)/shard_map/dot_general | solution.py:341
  69.1 110.4 %shard_map.47 = f32[256,512]{1,0:T(8,128)} custom-call(f32[256,512]{1,0:T(8,128)} %convolution_add_fusion.x_ref), custom_call_target="tpu_custom_call" | custom-call | tf_op jit(solution)/shard_map/pallas_call | solution.py:270
  179.6 1.9 %copy.15 = f32[256,512]{1,0:T(8,128)} copy(f32[256,512]{1,0:T(8,128)} %shard_map.47) | data formatting | bytes 1048576
Async XLA Ops:
  0.0 41.1 %copy-start = (bf16[2,40,128,128]{3,2,1,0:T(8,128)(2,1)S(1)}, bf16[2,40,128,128]{3,2,1,0:T(8,128)(2,1)}, u32[]{:S(2)}) copy-start(bf16[2,40,128,128]{3,2,1,0:T(8,128)(2,1)} %param.4) | copy-start | bytes 7864324
  32.1 29.5 %collective-permute-start = (bf16[2048,512]{1,0:T(8,128)(2,1)}, bf16[2048,512]{1,0:T(8,128)(2,1)}, u32[]{:S(2)}, u32[]{:S(2)}) collective-permute-start(bf16[2048,512]{1,0:T(8,128)(2,1)} %shard_map.46), channel_id=1, source_target_pairs={{0,8},{8,16},{16,24},{24,32},{32,40},{40,48},{48,56},{56,64},{64,7... | collective-permute-start | bytes 6291464 | tf_op jit(solution)/shard_map/ppermute | solution.py:306
  38.4 27.7 %collective-permute-start.1 = (bf16[2048,512]{1,0:T(8,128)(2,1)}, bf16[2048,512]{1,0:T(8,128)(2,1)}, u32[]{:S(2)}, u32[]{:S(2)}) collective-permute-start(bf16[2048,512]{1,0:T(8,128)(2,1)} %shard_map.46), channel_id=1, source_target_pairs={{8,0},{16,8},{24,16},{32,24},{40,32},{48,40},{56,48},{64,56},{72,6... | collective-permute-start | bytes 6291464 | tf_op jit(solution)/shard_map/ppermute | solution.py:307
  43.8 1.6 copy-start.1

commit v10 on v9

--- a/solution.py
+++ b/solution.py
@@ -208,7 +208,6 @@
     nb = n // t
     gram = g_ref[...] / count
     a_ref[...] = (gram + gram.T) / 2
-    m_ref[...] = jnp.zeros_like(m_ref)
     lane = lax.broadcasted_iota(jnp.int32, (1, t), 1)
     eye = (lax.broadcasted_iota(jnp.int32, (t, t), 0) == lax.broadcasted_iota(jnp.int32, (t, t), 1)).astype(jnp.float32)
 
@@ -265,7 +264,9 @@
 
         _ar_kernel(dims, gsc, None, rc, ry, rx, rzl, rzh, a1, a2, a3, a4, full, ssem, rsem, local_gram)
         _chol_inv_kernel(count, full, msc, ca, cd, cb, cl)
-        out_ref[...] = _mm_t(x_ref[...], msc[...])
+        for j in range(N // t):
+            k = (j + 1) * t
+            out_ref[:, j * t:k] = _mm_t(x_ref[:, :k], msc[j * t:k, :k])
 
     return pl.pallas_call(
         kernel,

time: 182 us -> 182 us (level)
  no operation moved by 1% of the time
where the time goes in v10:
time: 182 us
  Pallas kernels  143 us (79%)
  waiting for transfers between devices  17.7 us (10%)
  matrix products  8.75 us (5%)
  starting transfers between devices  8.16 us (4%)
  local copies, waits for them, and re-layouts  3.45 us (2%)
    pallas_call x1, Pallas kernels, orthonormal_basis(): pl.pallas_call(kernel, out_shape=jax.ShapeDtypeStruct(images.shape, jnp.f...  111 us
    pallas_call x1, Pallas kernels, zone_gather(): pl.pallas_call(functools.partial(_zone_gather_kernel, nb), out_shape=jax....  32.1 us
    ppermute x1, waiting for transfers between devices, extended(): before = lax.ppermute(last, axis, up)  15.6 us
    ppermute x1, starting transfers between devices, extended(): before = lax.ppermute(last, axis, up)  6.24 us
    dot_general x3, matrix products, add_columns(): jnp.dot(columns, shard_rows, preferred_element_type=jnp.float32)  6.08 us
  transfers between devices with their start and end apart: 2, of which 2 were waited for; matrix products, arithmetic and copies ran while one was open for 4% of the time, Pallas kernels for 0%

profile of v10, /device:TPU:1, one launch (start us, length us, event | category | flops | bytes accessed | tf_op | source)
XLA Modules:
  0.0 181.7 jit_solution(14888892670108934681)
XLA Ops:
  0.0 0.0 copy-start
  0.0 32.1 %shard_map.46 = bf16[2048,512]{1,0:T(8,128)(2,1)} custom-call(bf16[256,512]{1,0:T(8,128)(2,1)} %p_ref.1), custom_call_target="tpu_custom_call" | custom-call | tf_op jit(solution)/shard_map/pallas_call | solution.py:180
  32.1 6.2 %collective-permute-start = (bf16[2048,512]{1,0:T(8,128)(2,1)}, bf16[2048,512]{1,0:T(8,128)(2,1)}, u32[]{:S(2)}, u32[]{:S(2)}) collective-permute-start(bf16[2048,512]{1,0:T(8,128)(2,1)} %shard_map.46), channel_id=1, source_target_pairs={{0,8},{8,16},{16,24},{24,32},{32,40},{40,48},{48,56},{56,64},{64,7... | collective-permute-start | bytes 6291464 | tf_op jit(solution)/shard_map/ppermute | solution.py:307
  38.4 1.9 %collective-permute-start.1 = (bf16[2048,512]{1,0:T(8,128)(2,1)}, bf16[2048,512]{1,0:T(8,128)(2,1)}, u32[]{:S(2)}, u32[]{:S(2)}) collective-permute-start(bf16[2048,512]{1,0:T(8,128)(2,1)} %shard_map.46), channel_id=1, source_target_pairs={{8,0},{16,8},{24,16},{32,24},{40,32},{48,40},{56,48},{64,56},{72,6... | collective-permute-start | bytes 6291464 | tf_op jit(solution)/shard_map/ppermute | solution.py:308
  40.3 0.8 compare_and_fusion
  41.1 0.0 copy-done
  41.1 2.7 %fusion.2 = bf16[2,48,128,128]{3,1,2,0:T(8,128)(2,1)S(1)} fusion(bf16[2,40,128,128]{3,2,1,0:T(8,128)(2,1)S(1)} %copy-done, s32[2,40]{1,0:T(2,128)S(1)} %get-tuple-element.6, pred[2,40]{1,0:T(4,128)(4,1)S(1)} %get-tuple-element.5), kind=kOutput, calls=%fused_computation.3 | convolution fusion | flops 127409664 | bytes 5767568 | tf_op jit(solution)/shard_map/lsp,lsac->lapc/dot_general | solution.py:332
  43.8 0.0 copy-start.1
  43.8 0.8 copy.13
  44.6 0.8 copy-done.1
  45.3 0.7 fusion.7
  46.0 15.6 %collective-permute-done = bf16[2048,512]{1,0:T(8,128)(2,1)} collective-permute-done((bf16[2048,512]{1,0:T(8,128)(2,1)}, bf16[2048,512]{1,0:T(8,128)(2,1)}, u32[]{:S(2)}, u32[]{:S(2)}) %collective-permute-start) | collective-permute-done | bytes 2097184 | tf_op jit(solution)/shard_map/ppermute | solution.py:307
  61.6 2.3 %convolution_add_fusion.1 = f32[256,512]{1,0:T(8,128)S(1)} fusion(f32[256,512]{1,0:T(8,128)S(1)} %fusion.7, bf16[2048,512]{1,0:T(8,128)(2,1)} %collective-permute-done, bf16[256,6144]{1,0:T(8,128)(2,1)S(1)} %bitcast.16), kind=kOutput, calls=%fused_computation.5 | convolution fusion | flops 537001984 | bytes 4194304 | tf_op jit(solution)/shard_map/dot_general | solution.py:342
  63.9 2.1 %collective-permute-done.1 = bf16[2048,512]{1,0:T(8,128)(2,1)} collective-permute-done((bf16[2048,512]{1,0:T(8,128)(2,1)}, bf16[2048,512]{1,0:T(8,128)(2,1)}, u32[]{:S(2)}, u32[]{:S(2)}) %collective-permute-start.1) | collective-permute-done | bytes 2097184 | tf_op jit(solution)/shard_map/ppermute | solution.py:308
  66.0 3.1 %convolution_add_fusion.x_ref = f32[256,512]{1,0:T(8,128)} fusion(f32[256,512]{1,0:T(8,128)S(1)} %convolution_add_fusion.1, bf16[2048,512]{1,0:T(8,128)(2,1)} %collective-permute-done.1, bf16[256,6144]{1,0:T(8,128)(2,1)S(1)} %bitcast.17), kind=kOutput, calls=%fused_computation.4 | convolution fusion | flops 537001984 | bytes 4194304 | tf_op jit(solution)/shard_map/dot_general | solution.py:342
  69.1 110.7 %shard_map.47 = f32[256,512]{1,0:T(8,128)} custom-call(f32[256,512]{1,0:T(8,128)} %convolution_add_fusion.x_ref), custom_call_target="tpu_custom_call" | custom-call | tf_op jit(solution)/shard_map/pallas_call | solution.py:271
  179.8 1.9 %copy.15 = f32[256,512]{1,0:T(8,128)} copy(f32[256,512]{1,0:T(8,128)} %shard_map.47) | data formatting | bytes 1048576
Async XLA Ops:
  0.0 41.1 %copy-start = (bf16[2,40,128,128]{3,2,1,0:T(8,128)(2,1)S(1)}, bf16[2,40,128,128]{3,2,1,0:T(8,128)(2,1)}, u32[]{:S(2)}) copy-start(bf16[2,40,128,128]{3,2,1,0:T(8,128)(2,1)} %param.4) | copy-start | bytes 7864324
  32.1 29.5 %collective-permute-start = (bf16[2048,512]{1,0:T(8,128)(2,1)}, bf16[2048,512]{1,0:T(8,128)(2,1)}, u32[]{:S(2)}, u32[]{:S(2)}) collective-permute-start(bf16[2048,512]{1,0:T(8,128)(2,1)} %shard_map.46), channel_id=1, source_target_pairs={{0,8},{8,16},{16,24},{24,32},{32,40},{40,48},{48,56},{56,64},{64,7... | collective-permute-start | bytes 6291464 | tf_op jit(solution)/shard_map/ppermute | solution.py:307
  38.4 27.7 %collective-permute-start.1 = (bf16[2048,512]{1,0:T(8,128)(2,1)}, bf16[2048,512]{1,0:T(8,128)(2,1)}, u32[]{:S(2)}, u32[]{:S(2)}) collective-permute-start(bf16[2048,512]{1,0:T(8,128)(2,1)} %shard_map.46), channel_id=1, source_target_pairs={{8,0},{16,8},{24,16},{32,24},{40,32},{48,40},{56,48},{64,56},{72,6... | collective-permute-start | bytes 6291464 | tf_op jit(solution)/shard_map/ppermute | solution.py:308
  43.8 1.6 copy-start.1

commit v11 on v9

--- a/solution.py
+++ b/solution.py
@@ -52,11 +52,14 @@
     o_core, o_y, o_x, o_zl, o_zh = 0, 1, 1 + Y, 1 + Y + X, 2 + Y + X
     o_agzl, o_agx, o_agy, o_agc = 2 + Y + X + ZH, 3 + Y + X + ZH, 3 + Y + 2 * X + ZH, 3 + 2 * Y + 2 * X + ZH
 
+    pending = []
+
     def send(src, dst, sidx, ridx, peer):
         d = pltpu.make_async_remote_copy(
             src_ref=src, dst_ref=dst, send_sem=ssem.at[sidx], recv_sem=rsem.at[ridx],
             device_id=peer, device_id_type=MESH_ID)
         d.start()
+        pending.append(d)
         return d
 
     def wait_recv(src, dst, ridx, peer):
@@ -69,7 +72,6 @@
 
     d = send(g_ref.at[rows((1 - c) * S1, S1)], rc, o_core, o_core, core_peer)
     wait_recv(g_ref.at[rows(c * S1, S1)], rc, o_core, core_peer)
-    d.wait_send()
     a1[...] = g_ref[rows(c * S1, S1), :] + rc[...]
 
     ds = [send(a1.at[rows(p * S2, S2)], ry.at[y], o_y + k, o_y + y, dev(c, p, x, z))
@@ -77,8 +79,6 @@
     for k in range(1, Y):
         s = (y - k + Y) % Y
         wait_recv(a1.at[rows(0, S2)], ry.at[s], o_y + s, dev(c, s, x, z))
-    for d in ds:
-        d.wait_send()
     acc = a1[rows(y * S2, S2), :]
     for k in range(1, Y):
         acc = acc + ry[(y - k + Y) % Y]
@@ -89,8 +89,6 @@
     for k in range(1, X):
         s = (x - k + X) % X
         wait_recv(a2.at[rows(0, S3)], rx.at[s], o_x + s, dev(c, y, s, z))
-    for d in ds:
-        d.wait_send()
     acc = a2[rows(x * S3, S3), :]
     for k in range(1, X):
         acc = acc + rx[(x - k + X) % X]
@@ -98,7 +96,6 @@
 
     d = send(a3.at[rows((1 - zl) * S4, S4)], rzl, o_zl, o_zl, zl_peer)
     wait_recv(a3.at[rows(zl * S4, S4)], rzl, o_zl, zl_peer)
-    d.wait_send()
     a4[...] = a3[rows(zl * S4, S4), :] + rzl[...]
 
     ds = [send(a4, rzh.at[zh], o_zh + k, o_zh + zh, dev(c, y, x, p * 2 + zl))
@@ -107,8 +104,6 @@
     for k in range(1, ZH):
         s = (zh - k + ZH) % ZH
         wait_recv(a4, rzh.at[s], o_zh + s, dev(c, y, x, s * 2 + zl))
-    for d in ds:
-        d.wait_send()
     acc = rzh[0]
     for j in range(1, ZH):
         acc = acc + rzh[j]
@@ -118,7 +113,6 @@
     mine = rows(base + zl * S4, S4)
     d = send(full.at[mine], full.at[mine], o_agzl, o_agzl, zl_peer)
     wait_recv(full.at[mine], full.at[rows(base + (1 - zl) * S4, S4)], o_agzl, zl_peer)
-    d.wait_send()
 
     mine = rows(c * S1 + y * S2 + x * S3, S3)
     ds = [send(full.at[mine], full.at[mine], o_agx + k, o_agx + x, dev(c, y, p, z))
@@ -126,8 +120,6 @@
     for k in range(1, X):
         s = (x - k + X) % X
         wait_recv(full.at[mine], full.at[rows(c * S1 + y * S2 + s * S3, S3)], o_agx + s, dev(c, y, s, z))
-    for d in ds:
-        d.wait_send()
 
     mine = rows(c * S1 + y * S2, S2)
     ds = [send(full.at[mine], full.at[mine], o_agy + k, o_agy + y, dev(c, p, x, z))
@@ -135,14 +127,13 @@
     for k in range(1, Y):
         s = (y - k + Y) % Y
         wait_recv(full.at[mine], full.at[rows(c * S1 + s * S2, S2)], o_agy + s, dev(c, s, x, z))
-    for d in ds:
-        d.wait_send()
 
     mine = rows(c * S1, S1)
     d = send(full.at[mine], full.at[mine], o_agc, o_agc, core_peer)
     wait_recv(full.at[mine], full.at[rows((1 - c) * S1, S1)], o_agc, core_peer)
-    d.wait_send()
-
+
+    for d in pending:
+        d.wait_send()
     if out_ref is not None:
         out_ref[...] = full[...]
 

time: 182 us -> 182 us (level)
  no operation moved by 1% of the time
where the time goes in v11:
time: 182 us
  Pallas kernels  143 us (79%)
  waiting for transfers between devices  17.7 us (10%)
  matrix products  8.75 us (5%)
  starting transfers between devices  8.16 us (4%)
  local copies, waits for them, and re-layouts  3.45 us (2%)
    pallas_call x1, Pallas kernels, orthonormal_basis(): pl.pallas_call(kernel, out_shape=jax.ShapeDtypeStruct(images.shape, jnp.f...  111 us
    pallas_call x1, Pallas kernels, zone_gather(): pl.pallas_call(functools.partial(_zone_gather_kernel, nb), out_shape=jax....  32.1 us
    ppermute x1, waiting for transfers between devices, extended(): before = lax.ppermute(last, axis, up)  15.6 us
    ppermute x1, starting transfers between devices, extended(): before = lax.ppermute(last, axis, up)  6.24 us
    dot_general x3, matrix products, add_columns(): jnp.dot(columns, shard_rows, preferred_element_type=jnp.float32)  6.08 us
  transfers between devices with their start and end apart: 2, of which 2 were waited for; matrix products, arithmetic and copies ran while one was open for 4% of the time, Pallas kernels for 0%

profile of v11, /device:TPU:1, one launch (start us, length us, event | category | flops | bytes accessed | tf_op | source)
XLA Modules:
  0.0 181.6 jit_solution(12096737760107380987)
XLA Ops:
  0.0 0.0 copy-start
  0.0 32.1 %shard_map.46 = bf16[2048,512]{1,0:T(8,128)(2,1)} custom-call(bf16[256,512]{1,0:T(8,128)(2,1)} %p_ref.1), custom_call_target="tpu_custom_call" | custom-call | tf_op jit(solution)/shard_map/pallas_call | solution.py:171
  32.1 6.2 %collective-permute-start = (bf16[2048,512]{1,0:T(8,128)(2,1)}, bf16[2048,512]{1,0:T(8,128)(2,1)}, u32[]{:S(2)}, u32[]{:S(2)}) collective-permute-start(bf16[2048,512]{1,0:T(8,128)(2,1)} %shard_map.46), channel_id=1, source_target_pairs={{0,8},{8,16},{16,24},{24,32},{32,40},{40,48},{48,56},{56,64},{64,7... | collective-permute-start | bytes 6291464 | tf_op jit(solution)/shard_map/ppermute | solution.py:297
  38.4 1.9 %collective-permute-start.1 = (bf16[2048,512]{1,0:T(8,128)(2,1)}, bf16[2048,512]{1,0:T(8,128)(2,1)}, u32[]{:S(2)}, u32[]{:S(2)}) collective-permute-start(bf16[2048,512]{1,0:T(8,128)(2,1)} %shard_map.46), channel_id=1, source_target_pairs={{8,0},{16,8},{24,16},{32,24},{40,32},{48,40},{56,48},{64,56},{72,6... | collective-permute-start | bytes 6291464 | tf_op jit(solution)/shard_map/ppermute | solution.py:298
  40.3 0.8 compare_and_fusion
  41.1 0.0 copy-done
  41.1 2.7 %fusion.2 = bf16[2,48,128,128]{3,1,2,0:T(8,128)(2,1)S(1)} fusion(bf16[2,40,128,128]{3,2,1,0:T(8,128)(2,1)S(1)} %copy-done, s32[2,40]{1,0:T(2,128)S(1)} %get-tuple-element.6, pred[2,40]{1,0:T(4,128)(4,1)S(1)} %get-tuple-element.5), kind=kOutput, calls=%fused_computation.3 | convolution fusion | flops 127409664 | bytes 5767568 | tf_op jit(solution)/shard_map/lsp,lsac->lapc/dot_general | solution.py:322
  43.8 0.0 copy-start.1
  43.8 0.8 copy.13
  44.6 0.8 copy-done.1
  45.3 0.7 fusion.7
  46.0 15.6 %collective-permute-done = bf16[2048,512]{1,0:T(8,128)(2,1)} collective-permute-done((bf16[2048,512]{1,0:T(8,128)(2,1)}, bf16[2048,512]{1,0:T(8,128)(2,1)}, u32[]{:S(2)}, u32[]{:S(2)}) %collective-permute-start) | collective-permute-done | bytes 2097184 | tf_op jit(solution)/shard_map/ppermute | solution.py:297
  61.6 2.3 %convolution_add_fusion.1 = f32[256,512]{1,0:T(8,128)S(1)} fusion(f32[256,512]{1,0:T(8,128)S(1)} %fusion.7, bf16[2048,512]{1,0:T(8,128)(2,1)} %collective-permute-done, bf16[256,6144]{1,0:T(8,128)(2,1)S(1)} %bitcast.16), kind=kOutput, calls=%fused_computation.5 | convolution fusion | flops 537001984 | bytes 4194304 | tf_op jit(solution)/shard_map/dot_general | solution.py:332
  63.9 2.1 %collective-permute-done.1 = bf16[2048,512]{1,0:T(8,128)(2,1)} collective-permute-done((bf16[2048,512]{1,0:T(8,128)(2,1)}, bf16[2048,512]{1,0:T(8,128)(2,1)}, u32[]{:S(2)}, u32[]{:S(2)}) %collective-permute-start.1) | collective-permute-done | bytes 2097184 | tf_op jit(solution)/shard_map/ppermute | solution.py:298
  66.0 3.1 %convolution_add_fusion.x_ref = f32[256,512]{1,0:T(8,128)} fusion(f32[256,512]{1,0:T(8,128)S(1)} %convolution_add_fusion.1, bf16[2048,512]{1,0:T(8,128)(2,1)} %collective-permute-done.1, bf16[256,6144]{1,0:T(8,128)(2,1)S(1)} %bitcast.17), kind=kOutput, calls=%fused_computation.4 | convolution fusion | flops 537001984 | bytes 4194304 | tf_op jit(solution)/shard_map/dot_general | solution.py:332
  69.1 110.6 %shard_map.47 = f32[256,512]{1,0:T(8,128)} custom-call(f32[256,512]{1,0:T(8,128)} %convolution_add_fusion.x_ref), custom_call_target="tpu_custom_call" | custom-call | tf_op jit(solution)/shard_map/pallas_call | solution.py:261
  179.7 1.9 %copy.15 = f32[256,512]{1,0:T(8,128)} copy(f32[256,512]{1,0:T(8,128)} %shard_map.47) | data formatting | bytes 1048576
Async XLA Ops:
  0.0 41.1 %copy-start = (bf16[2,40,128,128]{3,2,1,0:T(8,128)(2,1)S(1)}, bf16[2,40,128,128]{3,2,1,0:T(8,128)(2,1)}, u32[]{:S(2)}) copy-start(bf16[2,40,128,128]{3,2,1,0:T(8,128)(2,1)} %param.4) | copy-start | bytes 7864324
  32.1 29.5 %collective-permute-start = (bf16[2048,512]{1,0:T(8,128)(2,1)}, bf16[2048,512]{1,0:T(8,128)(2,1)}, u32[]{:S(2)}, u32[]{:S(2)}) collective-permute-start(bf16[2048,512]{1,0:T(8,128)(2,1)} %shard_map.46), channel_id=1, source_target_pairs={{0,8},{8,16},{16,24},{24,32},{32,40},{40,48},{48,56},{56,64},{64,7... | collective-permute-start | bytes 6291464 | tf_op jit(solution)/shard_map/ppermute | solution.py:297
  38.4 27.7 %collective-permute-start.1 = (bf16[2048,512]{1,0:T(8,128)(2,1)}, bf16[2048,512]{1,0:T(8,128)(2,1)}, u32[]{:S(2)}, u32[]{:S(2)}) collective-permute-start(bf16[2048,512]{1,0:T(8,128)(2,1)} %shard_map.46), channel_id=1, source_target_pairs={{8,0},{16,8},{24,16},{32,24},{40,32},{48,40},{56,48},{64,56},{72,6... | collective-permute-start | bytes 6291464 | tf_op jit(solution)/shard_map/ppermute | solution.py:298
  43.8 1.6 copy-start.1
